TPU v7x, 256 devices: a whole 4x4x8 slice. The times are simulated.
256 devices in a mesh: member: 32 (over z_hi, y, core), tile: 8 (over x, z_lo).
Axes of the slice: x: 4, y: 4, z: 8 (z_hi: 4, z_lo: 2; z = z_hi * 2 + z_lo), core: 2. Of those that a mesh axis runs over, the one named last changes fastest.
Arguments:
- ensemble: float32 [64, 512, 4096], P('member', 'tile'), may hold values from -6 to 6
- velocity: float32 [2, 512, 4096], P(None, 'tile'), may hold values from -0.45 to 0.45
- observed_column: int32 [512, 32, 32], P('tile', 'member'), may hold values from 0 to 127
- observation_slot_count: int32 [512, 32], P('tile', 'member'), may hold values from 1 to 32
- local_radius: int32 [512, 32], P('tile', 'member'), may hold values from 16 to 128
- observed_value: float32 [512, 32, 32], P('tile', 'member'), may hold values from -9 to 9
- error_variance: float32 [512, 32, 32], P('tile', 'member'), may hold values from 0.25 to 2
Outputs:
- analysis: float32 [64, 512, 4096], P('member', 'tile')
All inputs are finite; a program needn't handle non-finite values.
Results may differ from a plain program's by a relative error of at most 0.0003.
Values sent between devices are 32-bit elements; how exact they have to be, the bound alone decides.
No kernel may reach another device: no remote copies, remote signals or barrier semaphores. Data moves between devices by JAX's collectives and lax.ppermute only.
A program may use at most 128 MiB of HBM per device.

v0:
```python
import functools

import jax
import jax.numpy as jnp
from jax import lax
from jax.experimental import pallas as pl
from jax.experimental.pallas import tpu as pltpu
from jax.sharding import PartitionSpec as P

COLS = 128
SWEEPS = 6
LANE = 128
BLOCK = 1024
GROUP = 4
SLOTS = 32
SIDE = 8


def stencil(window, first_col, last_col, rows_of):
    fields, wind_x, wind_y = window[:-2], window[-2], window[-1]
    rows, lanes = wind_x.shape
    face_x = 0.5 * (wind_x + pltpu.roll(wind_x, rows - 1, 0))
    before_x = pltpu.roll(face_x, 1, 0)
    face_y = 0.5 * (wind_y + pltpu.roll(wind_y, lanes - 1, 1))
    before_y = pltpu.roll(face_y, 1, 1)
    zero = jnp.zeros_like(face_x)
    centre = (
        1.0
        - jnp.maximum(face_x, 0.0)
        + jnp.minimum(before_x, 0.0)
        - jnp.maximum(face_y, 0.0)
        + jnp.minimum(before_y, 0.0)
    )
    row = lax.broadcasted_iota(jnp.int32, face_x.shape, 0)
    col = lax.broadcasted_iota(jnp.int32, face_x.shape, 1)
    low_row, high_row = rows_of
    north = jnp.where(row == low_row, zero, jnp.maximum(before_x, 0.0))
    south = jnp.where(row == high_row, zero, jnp.minimum(face_x, 0.0))
    west = jnp.where(col == first_col, zero, jnp.maximum(before_y, 0.0))
    east = jnp.where(col == last_col, zero, jnp.minimum(face_y, 0.0))
    out = []
    for field in fields:
        for _ in range(2):
            field = (
                centre * field
                + north * pltpu.roll(field, 1, 0)
                - south * pltpu.roll(field, rows - 1, 0)
                + west * pltpu.roll(field, 1, 1)
                - east * pltpu.roll(field, lanes - 1, 1)
            )
        out.append(field)
    return out


def advance(window_ref, out_ref, out_row, kept, low_row, high_row):
    width = window_ref.shape[2] - 2 * LANE
    count = BLOCK // LANE

    def step(k, carry):
        start = pl.multiple_of(k * BLOCK, BLOCK)
        window = [window_ref[i, :, pl.ds(start, BLOCK + 2 * LANE)] for i in range(4)]
        new = stencil(window, LANE - start, LANE - start + width - 1, (low_row, high_row))
        for m, field in enumerate(new):
            for t in range(count):
                out_ref[k * count + t, m, pl.ds(out_row, kept), :] = field[
                    SIDE : SIDE + kept, LANE * (t + 1) : LANE * (t + 2)
                ]
        return carry

    lax.fori_loop(0, width // BLOCK, step, 0)


def inner_kernel(ensemble_ref, velocity_ref, out_ref, window_ref, *, row0, kept):
    width = ensemble_ref.shape[2]
    rows = kept + 2 * SIDE
    pad = jnp.zeros((4, rows, LANE), jnp.float32)
    window_ref[:, :, pl.ds(0, LANE)] = pad
    window_ref[:, :, pl.ds(LANE + width, LANE)] = pad
    for i in range(2):
        window_ref[i, :, pl.ds(LANE, width)] = ensemble_ref[i, pl.ds(row0 - SIDE, rows), :]
        window_ref[2 + i, :, pl.ds(LANE, width)] = velocity_ref[i, pl.ds(row0 - SIDE, rows), :]
    advance(window_ref, out_ref, 0, kept, -1, -1)


def edge_kernel(edge_ref, ensemble_ref, velocity_ref, above_ref, below_ref, out_ref, window_ref, *, kept):
    height, width = ensemble_ref.shape[1:]
    rows = kept + 2 * SIDE
    pad = jnp.zeros((4, rows, LANE), jnp.float32)
    window_ref[:, :, pl.ds(0, LANE)] = pad
    window_ref[:, :, pl.ds(LANE + width, LANE)] = pad
    span = pl.ds(LANE, width)
    window_ref[:, pl.ds(0, SIDE), span] = jnp.zeros((4, SIDE, width), jnp.float32)
    window_ref[:, pl.ds(SIDE - 2, 2), span] = above_ref[...]
    for i in range(2):
        window_ref[i, pl.ds(SIDE, rows - SIDE), span] = ensemble_ref[i, pl.ds(0, rows - SIDE), :]
        window_ref[2 + i, pl.ds(SIDE, rows - SIDE), span] = velocity_ref[i, pl.ds(0, rows - SIDE), :]
    advance(window_ref, out_ref, 0, kept, jnp.where(edge_ref[0] == 1, SIDE, -1), -1)
    window_ref[:, pl.ds(rows - SIDE, SIDE), span] = jnp.zeros((4, SIDE, width), jnp.float32)
    window_ref[:, pl.ds(rows - SIDE, 2), span] = below_ref[...]
    first = height - (rows - SIDE)
    for i in range(2):
        window_ref[i, pl.ds(0, rows - SIDE), span] = ensemble_ref[i, pl.ds(first, rows - SIDE), :]
        window_ref[2 + i, pl.ds(0, rows - SIDE), span] = velocity_ref[i, pl.ds(first, rows - SIDE), :]
    advance(window_ref, out_ref, kept, kept, -1, jnp.where(edge_ref[1] == 1, SIDE + kept - 1, -1))


def vmem():
    return pl.BlockSpec(memory_space=pltpu.VMEM)


def forecast_inner(ensemble, velocity, row0, kept):
    members, _, width = ensemble.shape
    return pl.pallas_call(
        functools.partial(inner_kernel, row0=row0, kept=kept),
        out_shape=jax.ShapeDtypeStruct((width // COLS, members, kept, COLS), jnp.float32),
        in_specs=[vmem(), vmem()],
        out_specs=vmem(),
        scratch_shapes=[pltpu.VMEM((4, kept + 2 * SIDE, width + 2 * LANE), jnp.float32)],
        name="forecast_inner",
    )(ensemble, velocity)


def forecast_edge(edges, ensemble, velocity, above, below, kept):
    members, _, width = ensemble.shape
    return pl.pallas_call(
        functools.partial(edge_kernel, kept=kept),
        out_shape=jax.ShapeDtypeStruct((width // COLS, members, 2 * kept, COLS), jnp.float32),
        in_specs=[pl.BlockSpec(memory_space=pltpu.SMEM), vmem(), vmem(), vmem(), vmem()],
        out_specs=vmem(),
        scratch_shapes=[pltpu.VMEM((4, kept + 2 * SIDE, width + 2 * LANE), jnp.float32)],
        name="forecast_edge",
    )(edges, ensemble, velocity, above, below)


def split(x, parts=2):
    out = []
    for _ in range(parts - 1):
        out.append(x.astype(jnp.bfloat16))
        x = x - out[-1].astype(jnp.float32)
    return [*out, x.astype(jnp.bfloat16)]


def mm(a, b, dim=0):
    return lax.dot_general(a, b, (((1,), (dim,)), ((), ())), preferred_element_type=jnp.float32)


def product(left, right, dim=0):
    rows = left[0].shape[0]
    total = None
    for i in reversed(range(len(right))):
        kept = left[: len(right) - i]
        both = mm(jnp.concatenate(kept, axis=0), right[i], dim)
        for j in reversed(range(len(kept))):
            part = both[rows * j : rows * (j + 1)]
            total = part if total is None else total + part
    return total


def times(left, right):
    return product(split(left, len(right)), right)


def tile_of(ref, tile):
    members, tiles, width = ref.shape
    return ref.reshape(members * tiles, width).at[pl.ds(tile, members, stride=tiles), :]


def analysis_kernel(col_ref, root_ref, value_ref, x_ref, out_ref, *, groups):
    members = x_ref.shape[0]
    spare = members - 1.0
    wide = GROUP * members
    lane = lax.broadcasted_iota(jnp.int32, (1, LANE), 1)
    slots_of = [(lane // SLOTS) == b for b in range(GROUP)]

    def indicator(shape, row_size, col_size):
        row = lax.broadcasted_iota(jnp.int32, shape, 0) // row_size
        col = lax.broadcasted_iota(jnp.int32, shape, 1) // col_size
        return jnp.where(row == col, 1.0, 0.0).astype(jnp.bfloat16)

    block = indicator((wide, wide), members, members)
    slot_block = indicator((wide, LANE), members, SLOTS)
    eye = jnp.where(
        lax.broadcasted_iota(jnp.int32, (members, wide), 0)
        == lax.broadcasted_iota(jnp.int32, (members, wide), 1) % members,
        1.0,
        0.0,
    )
    spare_rows = jnp.zeros((15, wide), jnp.float32)

    def stacked(parts, mask):
        return [jnp.concatenate([part] * GROUP, axis=0) * mask for part in parts]

    def one(g):
        averages, anomalies = [], []
        spread = jnp.zeros((members, LANE), jnp.float32)
        there = jnp.zeros((8, LANE), jnp.float32)
        index = jnp.broadcast_to(col_ref[pl.ds(g, 1), :], (members, LANE))
        for b in range(GROUP):
            x = tile_of(x_ref, g * GROUP + b)[...]
            average = jnp.mean(x, axis=0, keepdims=True)
            anomaly = x - average
            averages.append(average)
            anomalies.append(anomaly)
            seen = jnp.take_along_axis(anomaly, index, axis=1, mode="promise_in_bounds")
            spread = jnp.where(slots_of[b], seen, spread)
            mean_seen = jnp.take_along_axis(
                jnp.broadcast_to(average, (8, LANE)), index[:8], axis=1, mode="promise_in_bounds"
            )
            there = jnp.where(slots_of[b], mean_seen, there)
        root = root_ref[pl.ds(g, 1), :]
        scaled = spread * root
        innovation = root * (value_ref[pl.ds(g, 1), :] - there[:1])
        yield
        scaled_split = split(scaled)
        wanted = jnp.concatenate([innovation, spare_rows[:, :LANE]], axis=0)
        left = [jnp.concatenate(pair, axis=0) for pair in zip(scaled_split, split(wanted))]
        stage = product(left, stacked(scaled_split, slot_block), 1)
        system = stage[:members] + spare * eye
        wanted = stage[members:]
        yield
        squares = jnp.sum(system * system, axis=0, keepdims=True)
        pieces = split(squares, 3) + [jnp.zeros((13, wide), jnp.bfloat16)]
        total = jnp.sum(mm(jnp.concatenate(pieces, axis=0), block), axis=0, keepdims=True)
        yield
        inverse = 1.0 / jnp.sqrt(total)
        root_norm = jnp.sqrt(inverse)
        system = system * inverse
        result = None
        for number in range(SWEEPS):
            factor = 1.5 * eye - 0.5 * system
            right = stacked(split(factor), block)
            last = number == SWEEPS - 1
            if last:
                stage = times(jnp.concatenate([result, wanted], axis=0), right)
                result, wanted = stage[:members], stage[members:]
            elif number == 0:
                stage = times(jnp.concatenate([system, wanted], axis=0), right)
                result, wanted = factor, stage[members:]
            else:
                stage = times(jnp.concatenate([system, result, wanted], axis=0), right)
                result, wanted = stage[members : 2 * members], stage[2 * members :]
            yield
            if not last:
                system = times(stage[:members], right)
                yield
        mean_weight = times(wanted, stacked(split(result), block))[:1] * inverse
        yield
        gain = split((spare**0.5 * root_norm) * result + mean_weight)
        high, low = split(jnp.concatenate(anomalies, axis=0))
        part = product(stacked(gain, block), [high, low])
        for b in range(GROUP):
            tile_of(out_ref, g * GROUP + b)[...] = part[members * b : members * (b + 1)] + averages[b]
        yield

    running = [one(g) for g in range(groups)]
    while running:
        running = [r for r in running if next(r, running) is None]


def analyse(background, columns, root_weight, values, groups):
    members, rows, width = background.shape
    tiles = groups * GROUP
    packed = lambda a: a.reshape(rows // tiles, groups, LANE)
    spec = pl.BlockSpec((None, groups, LANE), lambda i: (i, 0, 0))
    field = pl.BlockSpec((members, tiles, width), lambda i: (0, i, 0))
    return pl.pallas_call(
        functools.partial(analysis_kernel, groups=groups),
        grid=(rows // tiles,),
        out_shape=jax.ShapeDtypeStruct(background.shape, jnp.float32),
        in_specs=[spec, spec, spec, field],
        out_specs=field,
        name="analysis",
    )(packed(columns), packed(root_weight), packed(values), background)


def exchange(x):
    return lax.all_to_all(x, "member", 0, 0, tiled=True)


def per_device(ensemble, velocity, observed_column, slot_count, radius, observed_value, error_variance):
    members, height, width = ensemble.shape
    devices = lax.axis_size("tile")
    here = lax.axis_index("tile")
    edges = jnp.stack([here == 0, here == devices - 1]).astype(jnp.int32)
    up = [(i, i + 1) for i in range(devices - 1)]
    down = [(j, i) for i, j in up]
    above = lax.ppermute(
        jnp.concatenate([ensemble[:, -2:], velocity[:, -2:]], axis=0), "tile", up
    )
    below = lax.ppermute(jnp.concatenate([ensemble[:, :2], velocity[:, :2]], axis=0), "tile", down)

    columns = observed_column[:, 0]
    values = observed_value[:, 0]
    active = (jnp.arange(SLOTS, dtype=jnp.int32)[None, :] < slot_count).astype(jnp.float32)
    offset = (columns.astype(jnp.float32) - 0.5 * (COLS - 1)) / radius.astype(jnp.float32)
    root_weight = jnp.sqrt(active / (1.0 + offset * offset) / error_variance[:, 0])

    edge = height // 4
    kept = height - 2 * edge
    inner = slice(edge, height - edge)
    outer = lambda a, axis: jnp.concatenate(
        [lax.slice_in_dim(a, 0, edge, axis=axis), lax.slice_in_dim(a, height - edge, height, axis=axis)],
        axis=axis,
    )
    first = forecast_inner(ensemble, velocity, edge, kept)
    first, above, below = lax.optimization_barrier((first, above, below))
    first = exchange(first.reshape(-1, kept, COLS))
    second = exchange(forecast_edge(edges, ensemble, velocity, above, below, edge).reshape(-1, 2 * edge, COLS))
    first = analyse(first, columns[inner], root_weight[inner], values[inner], 2)
    first = exchange(first)
    second = analyse(second, outer(columns, 0), outer(root_weight, 0), outer(values, 0), 2)
    second = exchange(second)
    both = jnp.concatenate([second[:, :edge], first, second[:, edge:]], axis=1)
    both = both.reshape(-1, members, height, COLS)
    return both.transpose(1, 2, 0, 3).reshape(members, height, width)


def solution(mesh):
    return jax.shard_map(
        per_device,
        mesh=mesh,
        in_specs=(
            P("member", "tile", None),
            P(None, "tile", None),
            P("tile", "member", None),
            P("tile", "member"),
            P("tile", "member"),
            P("tile", "member", None),
            P("tile", "member", None),
        ),
        out_specs=P("member", "tile", None),
        check_vma=False,
    )
```

profile of v0, /device:TPU:7, one launch (start us, length us, event | category | flops | bytes accessed | tf_op | source)
XLA Modules:
  0.0 169.2 jit_solution(17648660168093733457)
XLA Ops:
  0.0 1.3 fusion.4
  1.4 3.5 %collective-permute-start = (f32[4,2,4096]{2,1,0:T(2,128)S(1)}, f32[4,2,4096]{2,1,0:T(2,128)S(1)}, u32[]{:S(2)}, u32[]{:S(2)}) collective-permute-start(f32[4,2,4096]{2,1,0:T(2,128)S(1)} %pad_maximum_fusion.1), channel_id=1, source_target_pairs={{0,1},{1,2},{2,3},{3,4},{4,5},{5,6},{6,7},{8,9},{9,10},{10,11},{11... | collective-permute-start | bytes 393224 | tf_op jit(solution)/shard_map/ppermute | solution.py:287
  5.0 2.6 %collective-permute-start.1 = (f32[4,2,4096]{2,1,0:T(2,128)S(1)}, f32[4,2,4096]{2,1,0:T(2,128)S(1)}, u32[]{:S(2)}, u32[]{:S(2)}) collective-permute-start(f32[4,2,4096]{2,1,0:T(2,128)S(1)} %pad_maximum_fusion.2), channel_id=1, source_target_pairs={{1,0},{2,1},{3,2},{4,3},{5,4},{6,5},{7,6},{9,8},{10,9},{11,10},{12... | collective-permute-start | bytes 393224 | tf_op jit(solution)/shard_map/ppermute | solution.py:290
  7.6 6.6 %forecast_inner.1 = f32[32,2,32,128]{3,2,1,0:T(8,128)} custom-call(f32[2,64,4096]{2,1,0:T(8,128)} %ensemble_ref.3, f32[2,64,4096]{2,1,0:T(8,128)} %velocity_ref.3), custom_call_target="tpu_custom_call" | custom-call | tf_op jit(solution)/shard_map/forecast_inner/pallas_call | solution.py:113
  14.2 0.7 add_convert_fusion.edge_ref
  14.9 0.6 copy-done.3
  15.5 0.6 copy-done.4
  16.2 8.1 %forecast_edge.1 = f32[32,2,32,128]{3,2,1,0:T(8,128)} custom-call(s32[2]{0:T(128)} %add_convert_fusion.edge_ref, f32[2,64,4096]{2,1,0:T(8,128)} %ensemble_ref.3, f32[2,64,4096]{2,1,0:T(8,128)} %velocity_ref.3, f32[4,2,4096]{2,1,0:T(2,128)} %copy-done.3, f32[4,2,4096]{2,1,0:T(2,128)} %copy-done.4), custom_call_target="tpu_custom_call" | custom-call | tf_op jit(solution)/shard_map/forecast_edge/pallas_call | solution.py:125
  24.3 41.4 %all_to_all.20.x_ref = f32[64,32,128]{2,1,0:T(8,128)} all-to-all(f32[64,32,128]{2,1,0:T(8,128)} %bitcast.41), channel_id=1, replica_groups=mesh['member'=32,'tile'=8] {'member'}, dimensions={0} | all-to-all | bytes 2097152 | tf_op jit(solution)/shard_map/all_to_all | solution.py:277
  65.7 5.4 %all-to-all-start.2 = ((f32[64,32,128]{2,1,0:T(8,128)}), f32[64,32,128]{2,1,0:T(8,128)S(1)}, u32[]{:S(2)}, u32[]{:S(2)}) async-start(f32[64,32,128]{2,1,0:T(8,128)} %bitcast.11), calls=%async_computation.2 | async-start | bytes 2097152 | tf_op jit(solution)/shard_map/all_to_all | solution.py:277
  71.3 0.7 reshape.42.root_ref
  72.3 0.7 reshape.43.value_ref
  73.2 0.7 reshape.41.col_ref
  73.8 14.5 %analysis.2 = f32[64,32,128]{2,1,0:T(8,128)} custom-call(s32[4,2,128]{2,1,0:T(2,128)} %reshape.41.col_ref, f32[4,2,128]{2,1,0:T(2,128)} %reshape.42.root_ref, f32[4,2,128]{2,1,0:T(2,128)} %reshape.43.value_ref, f32[64,32,128]{2,1,0:T(8,128)} %all_to_all.20.x_ref), custom_call_target="tpu_custom_call" | custom-call | tf_op jit(solution)/shard_map/analysis/pallas_call | solution.py:266
  88.4 11.2 %all-to-all-done.2.x_ref = f32[64,32,128]{2,1,0:T(8,128)S(1)} async-done(((f32[64,32,128]{2,1,0:T(8,128)}), f32[64,32,128]{2,1,0:T(8,128)S(1)}, u32[]{:S(2)}, u32[]{:S(2)}) %all-to-all-start.2) | async-done | bytes 1048608 | tf_op jit(solution)/shard_map/all_to_all | solution.py:277
  99.6 5.3 %all-to-all-start.1 = ((f32[64,32,128]{2,1,0:T(8,128)}), f32[64,32,128]{2,1,0:T(8,128)S(1)}, u32[]{:S(2)}, u32[]{:S(2)}) async-start(f32[64,32,128]{2,1,0:T(8,128)} %analysis.2), calls=%async_computation.1 | async-start | bytes 2097152 | tf_op jit(solution)/shard_map/all_to_all | solution.py:277
  105.2 0.7 reshape.46.root_ref
  106.0 0.7 reshape.47.value_ref
  106.7 0.7 reshape.45.col_ref
  107.4 14.6 %analysis.3 = f32[64,32,128]{2,1,0:T(8,128)} custom-call(s32[4,2,128]{2,1,0:T(2,128)} %reshape.45.col_ref, f32[4,2,128]{2,1,0:T(2,128)} %reshape.46.root_ref, f32[4,2,128]{2,1,0:T(2,128)} %reshape.47.value_ref, f32[64,32,128]{2,1,0:T(8,128)} %copy-done), custom_call_target="tpu_custom_call" | custom-call | tf_op jit(solution)/shard_map/analysis/pallas_call | solution.py:266
  122.0 11.5 %all-to-all-done.1 = f32[64,32,128]{2,1,0:T(8,128)S(1)} async-done(((f32[64,32,128]{2,1,0:T(8,128)}), f32[64,32,128]{2,1,0:T(8,128)S(1)}, u32[]{:S(2)}, u32[]{:S(2)}) %all-to-all-start.1) | async-done | bytes 1048608 | tf_op jit(solution)/shard_map/all_to_all | solution.py:277
  133.5 5.3 %all-to-all-start.3 = ((f32[64,32,128]{2,1,0:T(8,128)}), f32[64,32,128]{2,1,0:T(8,128)S(1)}, u32[]{:S(2)}, u32[]{:S(2)}) async-start(f32[64,32,128]{2,1,0:T(8,128)} %analysis.3), calls=%async_computation.3 | async-start | bytes 2097152 | tf_op jit(solution)/shard_map/all_to_all | solution.py:277
  138.9 28.5 %all-to-all-done.3 = f32[64,32,128]{2,1,0:T(8,128)S(1)} async-done(((f32[64,32,128]{2,1,0:T(8,128)}), f32[64,32,128]{2,1,0:T(8,128)S(1)}, u32[]{:S(2)}, u32[]{:S(2)}) %all-to-all-start.3) | async-done | bytes 1048608 | tf_op jit(solution)/shard_map/all_to_all | solution.py:277
  167.6 1.5 copy.17
  (37 shorter events, 1.6 us)
Async XLA Ops:
  1.4 13.5 %collective-permute-start = (f32[4,2,4096]{2,1,0:T(2,128)S(1)}, f32[4,2,4096]{2,1,0:T(2,128)S(1)}, u32[]{:S(2)}, u32[]{:S(2)}) collective-permute-start(f32[4,2,4096]{2,1,0:T(2,128)S(1)} %pad_maximum_fusion.1), channel_id=1, source_target_pairs={{0,1},{1,2},{2,3},{3,4},{4,5},{5,6},{6,7},{8,9},{9,10},{10,11},{11... | collective-permute-start | bytes 393224 | tf_op jit(solution)/shard_map/ppermute | solution.py:287
  5.0 9.9 %collective-permute-start.1 = (f32[4,2,4096]{2,1,0:T(2,128)S(1)}, f32[4,2,4096]{2,1,0:T(2,128)S(1)}, u32[]{:S(2)}, u32[]{:S(2)}) collective-permute-start(f32[4,2,4096]{2,1,0:T(2,128)S(1)} %pad_maximum_fusion.2), channel_id=1, source_target_pairs={{1,0},{2,1},{3,2},{4,3},{5,4},{6,5},{7,6},{9,8},{10,9},{11,10},{12... | collective-permute-start | bytes 393224 | tf_op jit(solution)/shard_map/ppermute | solution.py:290
  14.9 0.7 copy-start.3
  15.5 0.6 copy-start.4
  24.3 46.8 %copy-start.7 = (s32[64,1]{0,1:T(1,128)S(1)}, s32[64,1]{0,1:T(1,128)}, u32[]{:S(2)}) copy-start(s32[64,1]{0,1:T(1,128)} %param.11) | copy-start | bytes 772
  24.3 46.8 %copy-start.1 = (s32[64,1,32]{0,2,1:T(8,128)S(1)}, s32[64,1,32]{0,2,1:T(8,128)}, u32[]{:S(2)}) copy-start(s32[64,1,32]{0,2,1:T(8,128)} %param.9) | copy-start | bytes 24580
  24.3 46.8 %copy-start.5 = (f32[64,1,32]{0,2,1:T(8,128)S(1)}, f32[64,1,32]{0,2,1:T(8,128)}, u32[]{:S(2)}) copy-start(f32[64,1,32]{0,2,1:T(8,128)} %param.13) | copy-start | bytes 24580
  24.3 46.8 %copy-start.6 = (s32[64,1]{0,1:T(1,128)S(1)}, s32[64,1]{0,1:T(1,128)}, u32[]{:S(2)}) copy-start(s32[64,1]{0,1:T(1,128)} %param.10) | copy-start | bytes 772
  24.3 47.7 %copy-start.2 = (f32[64,1,32]{0,2,1:T(8,128)S(1)}, f32[64,1,32]{0,2,1:T(8,128)}, u32[]{:S(2)}) copy-start(f32[64,1,32]{0,2,1:T(8,128)} %param.12) | copy-start | bytes 24580
  65.7 33.9 %all-to-all-start.2 = ((f32[64,32,128]{2,1,0:T(8,128)}), f32[64,32,128]{2,1,0:T(8,128)S(1)}, u32[]{:S(2)}, u32[]{:S(2)}) async-start(f32[64,32,128]{2,1,0:T(8,128)} %bitcast.11), calls=%async_computation.2 | async-start | bytes 2097152 | tf_op jit(solution)/shard_map/all_to_all | solution.py:277
  99.6 7.8 %copy-start = (f32[64,32,128]{2,1,0:T(8,128)}, f32[64,32,128]{2,1,0:T(8,128)S(1)}, u32[]{:S(2)}) copy-start(f32[64,32,128]{2,1,0:T(8,128)S(1)} %all-to-all-done.2.x_ref) | copy-start | bytes 3145732
  99.6 33.9 %all-to-all-start.1 = ((f32[64,32,128]{2,1,0:T(8,128)}), f32[64,32,128]{2,1,0:T(8,128)S(1)}, u32[]{:S(2)}, u32[]{:S(2)}) async-start(f32[64,32,128]{2,1,0:T(8,128)} %analysis.2), calls=%async_computation.1 | async-start | bytes 2097152 | tf_op jit(solution)/shard_map/all_to_all | solution.py:277
  133.5 33.9 %all-to-all-start.3 = ((f32[64,32,128]{2,1,0:T(8,128)}), f32[64,32,128]{2,1,0:T(8,128)S(1)}, u32[]{:S(2)}, u32[]{:S(2)}) async-start(f32[64,32,128]{2,1,0:T(8,128)} %analysis.3), calls=%async_computation.3 | async-start | bytes 2097152 | tf_op jit(solution)/shard_map/all_to_all | solution.py:277
where the time goes:
time: 170 us; the launch traced here: 169 us
  waiting for transfers between devices  51.2 us (30%)
  Pallas kernels  43.8 us (26%)
  blocking collectives  41.4 us (24%)
  starting transfers between devices  22.2 us (13%)
  local copies, waits for them, and re-layouts  9.15 us (5%)
    all_to_all x3, waiting for transfers between devices, exchange(): return lax.all_to_all(x, 'member', 0, 0, tiled=True)  51.2 us
    all_to_all x1, blocking collectives, exchange(): return lax.all_to_all(x, 'member', 0, 0, tiled=True)  41.4 us
    pallas_call x2, Pallas kernels, analyse(): pl.pallas_call(functools.partial(analysis_kernel, groups=groups), grid=(r...  29.1 us
    all_to_all x3, starting transfers between devices, exchange(): return lax.all_to_all(x, 'member', 0, 0, tiled=True)  16 us
    pallas_call x1, Pallas kernels, forecast_edge(): pl.pallas_call(functools.partial(edge_kernel, kept=kept), out_shape=jax.S...  8.13 us
    pallas_call x1, Pallas kernels, forecast_inner(): pl.pallas_call(functools.partial(inner_kernel, row0=row0, kept=kept), out...  6.56 us
    reshape x6, local copies, waits for them, and re-layouts, analyse(): packed = lambda a: a.reshape(rows // tiles, groups, LANE)  4.07 us
    ppermute x1, starting transfers between devices, per_device(): lax.ppermute(jnp.concatenate([ensemble[:, -2:], velocity[:, -2:]], axis=0...  3.55 us
  transfers between devices with their start and end apart: 5, of which 3 were waited for; matrix products, arithmetic and copies ran while one was open for 4% of the time, Pallas kernels for 21%

commit v1 on v0

--- a/solution.py
+++ b/solution.py
@@ -10,14 +10,13 @@
 COLS = 128
 SWEEPS = 6
 LANE = 128
-BLOCK = 1024
+BLOCK = 2048
 GROUP = 4
 SLOTS = 32
 SIDE = 8
 
 
-def stencil(window, first_col, last_col, rows_of):
-    fields, wind_x, wind_y = window[:-2], window[-2], window[-1]
+def stencil(fields, wind_x, wind_y, first_col, last_col, low_row, high_row):
     rows, lanes = wind_x.shape
     face_x = 0.5 * (wind_x + pltpu.roll(wind_x, rows - 1, 0))
     before_x = pltpu.roll(face_x, 1, 0)
@@ -31,105 +30,107 @@
         - jnp.maximum(face_y, 0.0)
         + jnp.minimum(before_y, 0.0)
     )
+    north, south = jnp.maximum(before_x, 0.0), jnp.minimum(face_x, 0.0)
     row = lax.broadcasted_iota(jnp.int32, face_x.shape, 0)
+    if low_row is not None:
+        north = jnp.where(row == low_row, zero, north)
+    if high_row is not None:
+        south = jnp.where(row == high_row, zero, south)
     col = lax.broadcasted_iota(jnp.int32, face_x.shape, 1)
-    low_row, high_row = rows_of
-    north = jnp.where(row == low_row, zero, jnp.maximum(before_x, 0.0))
-    south = jnp.where(row == high_row, zero, jnp.minimum(face_x, 0.0))
     west = jnp.where(col == first_col, zero, jnp.maximum(before_y, 0.0))
     east = jnp.where(col == last_col, zero, jnp.minimum(face_y, 0.0))
-    out = []
-    for field in fields:
-        for _ in range(2):
-            field = (
-                centre * field
-                + north * pltpu.roll(field, 1, 0)
-                - south * pltpu.roll(field, rows - 1, 0)
-                + west * pltpu.roll(field, 1, 1)
-                - east * pltpu.roll(field, lanes - 1, 1)
-            )
-        out.append(field)
-    return out
-
-
-def advance(window_ref, out_ref, out_row, kept, low_row, high_row):
-    width = window_ref.shape[2] - 2 * LANE
-    count = BLOCK // LANE
-
-    def step(k, carry):
-        start = pl.multiple_of(k * BLOCK, BLOCK)
-        window = [window_ref[i, :, pl.ds(start, BLOCK + 2 * LANE)] for i in range(4)]
-        new = stencil(window, LANE - start, LANE - start + width - 1, (low_row, high_row))
-        for m, field in enumerate(new):
-            for t in range(count):
-                out_ref[k * count + t, m, pl.ds(out_row, kept), :] = field[
-                    SIDE : SIDE + kept, LANE * (t + 1) : LANE * (t + 2)
-                ]
-        return carry
-
-    lax.fori_loop(0, width // BLOCK, step, 0)
-
-
-def inner_kernel(ensemble_ref, velocity_ref, out_ref, window_ref, *, row0, kept):
-    width = ensemble_ref.shape[2]
-    rows = kept + 2 * SIDE
-    pad = jnp.zeros((4, rows, LANE), jnp.float32)
-    window_ref[:, :, pl.ds(0, LANE)] = pad
-    window_ref[:, :, pl.ds(LANE + width, LANE)] = pad
-    for i in range(2):
-        window_ref[i, :, pl.ds(LANE, width)] = ensemble_ref[i, pl.ds(row0 - SIDE, rows), :]
-        window_ref[2 + i, :, pl.ds(LANE, width)] = velocity_ref[i, pl.ds(row0 - SIDE, rows), :]
-    advance(window_ref, out_ref, 0, kept, -1, -1)
-
-
-def edge_kernel(edge_ref, ensemble_ref, velocity_ref, above_ref, below_ref, out_ref, window_ref, *, kept):
-    height, width = ensemble_ref.shape[1:]
-    rows = kept + 2 * SIDE
-    pad = jnp.zeros((4, rows, LANE), jnp.float32)
-    window_ref[:, :, pl.ds(0, LANE)] = pad
-    window_ref[:, :, pl.ds(LANE + width, LANE)] = pad
-    span = pl.ds(LANE, width)
-    window_ref[:, pl.ds(0, SIDE), span] = jnp.zeros((4, SIDE, width), jnp.float32)
-    window_ref[:, pl.ds(SIDE - 2, 2), span] = above_ref[...]
-    for i in range(2):
-        window_ref[i, pl.ds(SIDE, rows - SIDE), span] = ensemble_ref[i, pl.ds(0, rows - SIDE), :]
-        window_ref[2 + i, pl.ds(SIDE, rows - SIDE), span] = velocity_ref[i, pl.ds(0, rows - SIDE), :]
-    advance(window_ref, out_ref, 0, kept, jnp.where(edge_ref[0] == 1, SIDE, -1), -1)
-    window_ref[:, pl.ds(rows - SIDE, SIDE), span] = jnp.zeros((4, SIDE, width), jnp.float32)
-    window_ref[:, pl.ds(rows - SIDE, 2), span] = below_ref[...]
-    first = height - (rows - SIDE)
-    for i in range(2):
-        window_ref[i, pl.ds(0, rows - SIDE), span] = ensemble_ref[i, pl.ds(first, rows - SIDE), :]
-        window_ref[2 + i, pl.ds(0, rows - SIDE), span] = velocity_ref[i, pl.ds(first, rows - SIDE), :]
-    advance(window_ref, out_ref, kept, kept, -1, jnp.where(edge_ref[1] == 1, SIDE + kept - 1, -1))
-
-
-def vmem():
-    return pl.BlockSpec(memory_space=pltpu.VMEM)
+
+    def substep(field, part):
+        return (
+            centre[part] * field[part]
+            + north[part] * pltpu.roll(field, 1, 0)[part]
+            - south[part] * pltpu.roll(field, rows - 1, 0)[part]
+            + west[part] * pltpu.roll(field, 1, 1)[part]
+            - east[part] * pltpu.roll(field, lanes - 1, 1)[part]
+        )
+
+    kept = (slice(SIDE, rows - SIDE), slice(LANE, lanes - LANE))
+    return [substep(substep(field, (slice(None), slice(None))), kept) for field in fields]
+
+
+def advance(pieces, out_ref, out_row, low_row, high_row):
+    k, last = pl.program_id(0), pl.num_programs(0) - 1
+    *fields, wind_x, wind_y = pieces
+    rows, lanes = wind_x.shape
+    inside_left = jnp.where(k > 0, wind_y[:, :LANE], 0.0)
+    inside_right = jnp.where(k < last, wind_y[:, lanes - LANE :], 0.0)
+    wind_y = jnp.concatenate([inside_left, wind_y[:, LANE : lanes - LANE], inside_right], axis=1)
+    first_col = jnp.where(k == 0, LANE, -1)
+    last_col = jnp.where(k == last, lanes - LANE - 1, -1)
+    new = stencil(fields, wind_x, wind_y, first_col, last_col, low_row, high_row)
+    for m, field in enumerate(new):
+        for t in range(field.shape[1] // LANE):
+            out_ref[t, m, pl.ds(out_row, rows - 2 * SIDE), :] = field[:, LANE * t : LANE * (t + 1)]
+
+
+def joined(refs, i, rows):
+    return jnp.concatenate([ref[i, rows, :] for ref in refs], axis=1)
+
+
+def inner_kernel(*refs, row0, kept):
+    *refs, out_ref = refs
+    rows = slice(row0 - SIDE, row0 + kept + SIDE)
+    advance([joined(refs[3 * (i // 2) : 3 * (i // 2) + 3], i % 2, rows) for i in range(4)], out_ref, 0, None, None)
+
+
+def edge_kernel(edge_ref, *refs, kept):
+    *refs, out_ref = refs
+    height = refs[0].shape[1]
+    far = jnp.zeros((SIDE - 2, out_ref.shape[0] * LANE + 2 * LANE), jnp.float32)
+    body = lambda i, rows: joined(refs[3 * (i // 2) : 3 * (i // 2) + 3], i % 2, rows)
+    beyond = lambda j, i: joined(refs[6 + 3 * j : 9 + 3 * j], i, slice(None))
+    top = [
+        jnp.concatenate([far, beyond(0, i), body(i, slice(0, kept + SIDE))], axis=0) for i in range(4)
+    ]
+    advance(top, out_ref, 0, jnp.where(edge_ref[0] == 1, SIDE, -1), None)
+    bottom = [
+        jnp.concatenate([body(i, slice(height - kept - SIDE, height)), beyond(1, i), far], axis=0)
+        for i in range(4)
+    ]
+    advance(bottom, out_ref, kept, None, jnp.where(edge_ref[1] == 1, SIDE + kept - 1, -1))
+
+
+def around(count, height, width):
+    per, last = BLOCK // LANE, width // LANE - 1
+    return [
+        pl.BlockSpec((count, height, LANE), lambda k: (0, 0, jnp.maximum(per * k - 1, 0))),
+        pl.BlockSpec((count, height, BLOCK), lambda k: (0, 0, k)),
+        pl.BlockSpec((count, height, LANE), lambda k: (0, 0, jnp.minimum(per * (k + 1), last))),
+    ]
 
 
 def forecast_inner(ensemble, velocity, row0, kept):
-    members, _, width = ensemble.shape
+    members, height, width = ensemble.shape
+    per = BLOCK // LANE
     return pl.pallas_call(
         functools.partial(inner_kernel, row0=row0, kept=kept),
+        grid=(width // BLOCK,),
         out_shape=jax.ShapeDtypeStruct((width // COLS, members, kept, COLS), jnp.float32),
-        in_specs=[vmem(), vmem()],
-        out_specs=vmem(),
-        scratch_shapes=[pltpu.VMEM((4, kept + 2 * SIDE, width + 2 * LANE), jnp.float32)],
+        in_specs=around(members, height, width) + around(2, height, width),
+        out_specs=pl.BlockSpec((per, members, kept, COLS), lambda k: (k, 0, 0, 0)),
         name="forecast_inner",
-    )(ensemble, velocity)
+    )(*[ensemble] * 3, *[velocity] * 3)
 
 
 def forecast_edge(edges, ensemble, velocity, above, below, kept):
-    members, _, width = ensemble.shape
+    members, height, width = ensemble.shape
+    per = BLOCK // LANE
     return pl.pallas_call(
         functools.partial(edge_kernel, kept=kept),
+        grid=(width // BLOCK,),
         out_shape=jax.ShapeDtypeStruct((width // COLS, members, 2 * kept, COLS), jnp.float32),
-        in_specs=[pl.BlockSpec(memory_space=pltpu.SMEM), vmem(), vmem(), vmem(), vmem()],
-        out_specs=vmem(),
-        scratch_shapes=[pltpu.VMEM((4, kept + 2 * SIDE, width + 2 * LANE), jnp.float32)],
+        in_specs=[pl.BlockSpec(memory_space=pltpu.SMEM)]
+        + around(members, height, width)
+        + around(2, height, width)
+        + around(4, 2, width) * 2,
+        out_specs=pl.BlockSpec((per, members, 2 * kept, COLS), lambda k: (k, 0, 0, 0)),
         name="forecast_edge",
-    )(edges, ensemble, velocity, above, below)
+    )(edges, *[ensemble] * 3, *[velocity] * 3, *[above] * 3, *[below] * 3)
 
 
 def split(x, parts=2):
@@ -257,20 +258,27 @@
         running = [r for r in running if next(r, running) is None]
 
 
-def analyse(background, columns, root_weight, values, groups):
+def analyse(background, observations, groups, total, first_block, earlier=None):
     members, rows, width = background.shape
     tiles = groups * GROUP
-    packed = lambda a: a.reshape(rows // tiles, groups, LANE)
+    packed = [a.reshape(rows // tiles, groups, LANE) for a in observations]
     spec = pl.BlockSpec((None, groups, LANE), lambda i: (i, 0, 0))
-    field = pl.BlockSpec((members, tiles, width), lambda i: (0, i, 0))
+    field = lambda shift: pl.BlockSpec((members, tiles, width), lambda i: (0, i + shift, 0))
+    kernel = functools.partial(analysis_kernel, groups=groups)
+    more = {}
+    if earlier is not None:
+        inner = kernel
+        kernel = lambda a, b, c, x, _, out: inner(a, b, c, x, out)
+        more = {"input_output_aliases": {4: 0}}
     return pl.pallas_call(
-        functools.partial(analysis_kernel, groups=groups),
+        kernel,
         grid=(rows // tiles,),
-        out_shape=jax.ShapeDtypeStruct(background.shape, jnp.float32),
-        in_specs=[spec, spec, spec, field],
-        out_specs=field,
+        out_shape=jax.ShapeDtypeStruct((members, total, width), jnp.float32),
+        in_specs=[spec, spec, spec, field(0)] + [pl.BlockSpec(memory_space=pl.ANY)] * len(more),
+        out_specs=field(first_block),
         name="analysis",
-    )(packed(columns), packed(root_weight), packed(values), background)
+        **more,
+    )(*packed, background, *([] if earlier is None else [earlier]))
 
 
 def exchange(x):
@@ -281,36 +289,35 @@
     members, height, width = ensemble.shape
     devices = lax.axis_size("tile")
     here = lax.axis_index("tile")
-    edges = jnp.stack([here == 0, here == devices - 1]).astype(jnp.int32)
     up = [(i, i + 1) for i in range(devices - 1)]
     down = [(j, i) for i, j in up]
-    above = lax.ppermute(
-        jnp.concatenate([ensemble[:, -2:], velocity[:, -2:]], axis=0), "tile", up
+    edge = height // 8
+    kept = height - 2 * edge
+    blocks = kept // (4 * GROUP)
+    inner = slice(edge, height - edge)
+    outer = lambda a, axis: jnp.concatenate(
+        [lax.slice_in_dim(a, 0, edge, axis=axis), lax.slice_in_dim(a, height - edge, height, axis=axis)],
+        axis=axis,
     )
-    below = lax.ppermute(jnp.concatenate([ensemble[:, :2], velocity[:, :2]], axis=0), "tile", down)
-
     columns = observed_column[:, 0]
     values = observed_value[:, 0]
     active = (jnp.arange(SLOTS, dtype=jnp.int32)[None, :] < slot_count).astype(jnp.float32)
     offset = (columns.astype(jnp.float32) - 0.5 * (COLS - 1)) / radius.astype(jnp.float32)
     root_weight = jnp.sqrt(active / (1.0 + offset * offset) / error_variance[:, 0])
-
-    edge = height // 4
-    kept = height - 2 * edge
-    inner = slice(edge, height - edge)
-    outer = lambda a, axis: jnp.concatenate(
-        [lax.slice_in_dim(a, 0, edge, axis=axis), lax.slice_in_dim(a, height - edge, height, axis=axis)],
-        axis=axis,
-    )
+    inner_obs = [a[inner] for a in (columns, root_weight, values)]
+    outer_obs = [outer(a, 0) for a in (columns, root_weight, values)]
+    edges = jnp.stack([here == 0, here == devices - 1]).astype(jnp.int32)
+
     first = forecast_inner(ensemble, velocity, edge, kept)
-    first, above, below = lax.optimization_barrier((first, above, below))
     first = exchange(first.reshape(-1, kept, COLS))
-    second = exchange(forecast_edge(edges, ensemble, velocity, above, below, edge).reshape(-1, 2 * edge, COLS))
-    first = analyse(first, columns[inner], root_weight[inner], values[inner], 2)
-    first = exchange(first)
-    second = analyse(second, outer(columns, 0), outer(root_weight, 0), outer(values, 0), 2)
-    second = exchange(second)
-    both = jnp.concatenate([second[:, :edge], first, second[:, edge:]], axis=1)
+    above = lax.ppermute(jnp.concatenate([ensemble[:, -2:], velocity[:, -2:]], axis=0), "tile", up)
+    below = lax.ppermute(jnp.concatenate([ensemble[:, :2], velocity[:, :2]], axis=0), "tile", down)
+    second = forecast_edge(edges, ensemble, velocity, above, below, edge)
+    second = exchange(second.reshape(-1, 2 * edge, COLS))
+    done = analyse(first, inner_obs, 4, height, 0)
+    done = analyse(second, outer_obs, 4, height, blocks, done)
+    done = exchange(done)
+    both = jnp.concatenate([done[:, kept : kept + edge], done[:, :kept], done[:, kept + edge :]], axis=1)
     both = both.reshape(-1, members, height, COLS)
     return both.transpose(1, 2, 0, 3).reshape(members, height, width)
 

time: 170 us -> 164 us (0.965)
  waiting for transfers between devices: 51.2 us -> 31.5 us
  blocking collectives: 41.4 us -> 61 us
  Pallas kernels: 43.8 us -> 30.4 us
  starting transfers between devices: 22.2 us -> 27.9 us
    all_to_all x3 -> x2, waiting for transfers between devices: 51.2 us -> 0.01 us  [exchange(): return lax.all_to_all(x, 'member', 0, 0, tiled=True)]
    ppermute x1, waiting for transfers between devices: 0.01 us -> 30.4 us  [per_device(): lax.ppermute(jnp.concatenate([ensemble[:, -2:], velocity[:, -2:]], axis=0...]
    all_to_all x1, blocking collectives: 41.4 us -> 61 us  [exchange(): return lax.all_to_all(x, 'member', 0, 0, tiled=True)]
    pallas_call x4, Pallas kernels: 43.8 us -> 30.4 us  [the longest x2 18.8 us: analyse(): pl.pallas_call(kernel, grid=(rows // tiles,), out_shape=jax.ShapeDtypeStr...]
    all_to_all x3 -> x2, starting transfers between devices: 16 us -> 21.7 us  [exchange(): return lax.all_to_all(x, 'member', 0, 0, tiled=True)]
  transfers between devices with their start and end apart: 5 -> 4, of which waited for: 3 -> 2; matrix products, arithmetic and copies ran while one was open for 4% -> 4% of each run, Pallas kernels for 21% -> 11%
where the time goes in v1:
time: 164 us; the launch traced here: 161 us
  blocking collectives  61 us (37%)
  waiting for transfers between devices  31.5 us (19%)
  Pallas kernels  30.4 us (19%)
  starting transfers between devices  27.9 us (17%)
  local copies, waits for them, and re-layouts  9.35 us (6%)
    all_to_all x1, blocking collectives, exchange(): return lax.all_to_all(x, 'member', 0, 0, tiled=True)  61 us
    ppermute x1, waiting for transfers between devices, per_device(): lax.ppermute(jnp.concatenate([ensemble[:, -2:], velocity[:, -2:]], axis=0...  30.4 us
    all_to_all x2, starting transfers between devices, exchange(): return lax.all_to_all(x, 'member', 0, 0, tiled=True)  21.7 us
    pallas_call x2, Pallas kernels, analyse(): pl.pallas_call(kernel, grid=(rows // tiles,), out_shape=jax.ShapeDtypeStr...  18.8 us
    pallas_call x1, Pallas kernels, forecast_inner(): pl.pallas_call(functools.partial(inner_kernel, row0=row0, kept=kept), gri...  6.35 us
    pallas_call x1, Pallas kernels, forecast_edge(): pl.pallas_call(functools.partial(edge_kernel, kept=kept), grid=(width //...  5.26 us
    reshape x6, local copies, waits for them, and re-layouts, analyse(): packed = [a.reshape(rows // tiles, groups, LANE) for a in observations]  4.03 us
    ppermute x1, starting transfers between devices, per_device(): lax.ppermute(jnp.concatenate([ensemble[:, :2], velocity[:, :2]], axis=0),...  3.53 us
  transfers between devices with their start and end apart: 4, of which 2 were waited for; matrix products, arithmetic and copies ran while one was open for 4% of the time, Pallas kernels for 11%

profile of v1, /device:TPU:7, one launch (start us, length us, event | category | flops | bytes accessed | tf_op | source)
XLA Modules:
  0.0 161.5 jit_solution(11187838698834557460)
XLA Ops:
  0.0 6.4 %forecast_inner.1 = f32[32,2,48,128]{3,2,1,0:T(8,128)} custom-call(f32[2,64,4096]{2,1,0:T(8,128)} %refs_2_.3, f32[2,64,4096]{2,1,0:T(8,128)} %refs_2_.3, f32[2,64,4096]{2,1,0:T(8,128)} %refs_2_.3, f32[2,64,4096]{2,1,0:T(8,128)} %refs_5_.3, f32[2,64,4096]{2,1,0:T(8,128)} %refs_5_.3, f32[2,64,4096]{2,1,0:T(8,128)} %refs_5_.3), custom_call_target="tpu_custom_call" | custom-call | tf_op jit(solution)/shard_map/forecast_inner/pallas_call | solution.py:110
  6.4 12.1 %all-to-all-start.1 = ((f32[64,48,128]{2,1,0:T(8,128)}), f32[64,48,128]{2,1,0:T(8,128)S(1)}, u32[]{:S(2)}, u32[]{:S(2)}) async-start(f32[64,48,128]{2,1,0:T(8,128)} %bitcast.41), calls=%async_computation.1 | async-start | bytes 3145728 | tf_op jit(solution)/shard_map/all_to_all | solution.py:285
  18.4 1.3 fusion.5
  19.8 2.6 %collective-permute-start = (f32[4,2,4096]{2,1,0:T(2,128)S(1)}, f32[4,2,4096]{2,1,0:T(2,128)S(1)}, u32[]{:S(2)}, u32[]{:S(2)}) collective-permute-start(f32[4,2,4096]{2,1,0:T(2,128)S(1)} %pad_maximum_fusion.1), channel_id=1, source_target_pairs={{0,1},{1,2},{2,3},{3,4},{4,5},{5,6},{6,7},{8,9},{9,10},{10,11},{11... | collective-permute-start | bytes 393224 | tf_op jit(solution)/shard_map/ppermute | solution.py:313
  22.5 3.5 %collective-permute-start.1 = (f32[4,2,4096]{2,1,0:T(2,128)S(1)}, f32[4,2,4096]{2,1,0:T(2,128)S(1)}, u32[]{:S(2)}, u32[]{:S(2)}) collective-permute-start(f32[4,2,4096]{2,1,0:T(2,128)S(1)} %pad_maximum_fusion.2), channel_id=1, source_target_pairs={{1,0},{2,1},{3,2},{4,3},{5,4},{6,5},{7,6},{9,8},{10,9},{11,10},{12... | collective-permute-start | bytes 393224 | tf_op jit(solution)/shard_map/ppermute | solution.py:314
  26.1 0.6 add_convert_fusion.edge_ref
  26.7 30.4 %collective-permute-done.refs_6_.refs_7_.refs_8_ = f32[4,2,4096]{2,1,0:T(2,128)S(1)} collective-permute-done((f32[4,2,4096]{2,1,0:T(2,128)S(1)}, f32[4,2,4096]{2,1,0:T(2,128)S(1)}, u32[]{:S(2)}, u32[]{:S(2)}) %collective-permute-start) | collective-permute-done | bytes 131104 | tf_op jit(solution)/shard_map/ppermute | solution.py:313
  57.0 1.1 collective-permute-done.1.refs_9_.refs_10_.refs_11_
  58.1 0.6 copy-done.3
  58.8 5.3 %forecast_edge.1 = f32[32,2,16,128]{3,2,1,0:T(8,128)} custom-call(s32[2]{0:T(128)} %add_convert_fusion.edge_ref, f32[2,64,4096]{2,1,0:T(8,128)} %refs_2_.3, f32[2,64,4096]{2,1,0:T(8,128)} %refs_2_.3, f32[2,64,4096]{2,1,0:T(8,128)} %refs_2_.3, f32[2,64,4096]{2,1,0:T(8,128)} %refs_5_.3, f32[2,64,4096]{2,1,0:T(8,128)} %refs_5_.3, f32[2,64,4096]{2,1,0:T(8,128)} %refs_5_.3, ...), custom_call_target="tpu_custom_call" | custom-call | tf_op jit(solution)/shard_map/forecast_edge/pallas_call | solution.py:123
  64.1 9.6 %all-to-all-start = ((f32[64,16,128]{2,1,0:T(8,128)}), f32[64,16,128]{2,1,0:T(8,128)S(1)}, u32[]{:S(2)}, u32[]{:S(2)}) async-start(f32[64,16,128]{2,1,0:T(8,128)} %bitcast.42), calls=%async_computation | async-start | bytes 1048576 | tf_op jit(solution)/shard_map/all_to_all | solution.py:285
  74.0 0.7 reshape.46.root_ref
  74.8 0.7 reshape.47.value_ref
  75.6 0.7 reshape.45.col_ref
  76.5 0.7 reshape.42.b
  77.4 0.7 reshape.43.c
  78.3 0.7 reshape.41.a
  78.9 13.2 %analysis.2._ = f32[64,64,128]{2,1,0:T(8,128)} custom-call(s32[3,4,128]{2,1,0:T(4,128)} %reshape.45.col_ref, f32[3,4,128]{2,1,0:T(4,128)} %reshape.46.root_ref, f32[3,4,128]{2,1,0:T(4,128)} %reshape.47.value_ref, f32[64,48,128]{2,1,0:T(8,128)} %copy-done), custom_call_target="tpu_custom_call" | custom-call | tf_op jit(solution)/shard_map/analysis/pallas_call | solution.py:273
  92.1 0.8 copy-done.1
  92.9 5.6 %analysis.3 = f32[64,64,128]{2,1,0:T(8,128)} custom-call(s32[1,4,128]{2,1,0:T(4,128)} %reshape.41.a, f32[1,4,128]{2,1,0:T(4,128)} %reshape.42.b, f32[1,4,128]{2,1,0:T(4,128)} %reshape.43.c, f32[64,16,128]{2,1,0:T(8,128)} %copy-done.1, f32[64,64,128]{2,1,0:T(8,128)} %analysis.2._), custom_call_target="tpu_custom_call", output_to_operand_aliasing={{}: (4, {})} | custom-call | tf_op jit(solution)/shard_map/analysis/pallas_call | solution.py:273
  98.5 61.0 %all_to_all.15 = f32[64,64,128]{2,1,0:T(8,128)S(1)} all-to-all(f32[64,64,128]{2,1,0:T(8,128)} %analysis.3), channel_id=1, replica_groups=mesh['member'=32,'tile'=8] {'member'}, dimensions={0} | all-to-all | bytes 4194304 | tf_op jit(solution)/shard_map/all_to_all | solution.py:285
  159.6 0.1 slice.86
  159.7 0.3 pad_maximum_fusion
  160.0 1.5 copy.25
  (38 shorter events, 1.3 us)
Async XLA Ops:
  6.4 19.7 %copy-start.8 = (s32[64,1]{0,1:T(1,128)S(1)}, s32[64,1]{0,1:T(1,128)}, u32[]{:S(2)}) copy-start(s32[64,1]{0,1:T(1,128)} %param.11) | copy-start | bytes 772
  6.4 57.7 %all-to-all-start.1 = ((f32[64,48,128]{2,1,0:T(8,128)}), f32[64,48,128]{2,1,0:T(8,128)S(1)}, u32[]{:S(2)}, u32[]{:S(2)}) async-start(f32[64,48,128]{2,1,0:T(8,128)} %bitcast.41), calls=%async_computation.1 | async-start | bytes 3145728 | tf_op jit(solution)/shard_map/all_to_all | solution.py:285
  19.8 37.3 %collective-permute-start = (f32[4,2,4096]{2,1,0:T(2,128)S(1)}, f32[4,2,4096]{2,1,0:T(2,128)S(1)}, u32[]{:S(2)}, u32[]{:S(2)}) collective-permute-start(f32[4,2,4096]{2,1,0:T(2,128)S(1)} %pad_maximum_fusion.1), channel_id=1, source_target_pairs={{0,1},{1,2},{2,3},{3,4},{4,5},{5,6},{6,7},{8,9},{9,10},{10,11},{11... | collective-permute-start | bytes 393224 | tf_op jit(solution)/shard_map/ppermute | solution.py:313
  22.5 35.6 %collective-permute-start.1 = (f32[4,2,4096]{2,1,0:T(2,128)S(1)}, f32[4,2,4096]{2,1,0:T(2,128)S(1)}, u32[]{:S(2)}, u32[]{:S(2)}) collective-permute-start(f32[4,2,4096]{2,1,0:T(2,128)S(1)} %pad_maximum_fusion.2), channel_id=1, source_target_pairs={{1,0},{2,1},{3,2},{4,3},{5,4},{6,5},{7,6},{9,8},{10,9},{11,10},{12... | collective-permute-start | bytes 393224 | tf_op jit(solution)/shard_map/ppermute | solution.py:314
  26.6 47.1 %copy-start.4 = (s32[64,1,32]{0,2,1:T(8,128)S(1)}, s32[64,1,32]{0,2,1:T(8,128)}, u32[]{:S(2)}) copy-start(s32[64,1,32]{0,2,1:T(8,128)} %param.9) | copy-start | bytes 24580
  26.7 47.1 %copy-start.6 = (f32[64,1,32]{0,2,1:T(8,128)S(1)}, f32[64,1,32]{0,2,1:T(8,128)}, u32[]{:S(2)}) copy-start(f32[64,1,32]{0,2,1:T(8,128)} %param.13) | copy-start | bytes 24580
  26.7 47.1 %copy-start.7 = (s32[64,1]{0,1:T(1,128)S(1)}, s32[64,1]{0,1:T(1,128)}, u32[]{:S(2)}) copy-start(s32[64,1]{0,1:T(1,128)} %param.10) | copy-start | bytes 772
  26.7 48.0 %copy-start.5 = (f32[64,1,32]{0,2,1:T(8,128)S(1)}, f32[64,1,32]{0,2,1:T(8,128)}, u32[]{:S(2)}) copy-start(f32[64,1,32]{0,2,1:T(8,128)} %param.12) | copy-start | bytes 24580
  57.0 1.1 copy-start.2
  58.1 0.6 copy-start.3
  64.1 14.9 %copy-start = (f32[64,48,128]{2,1,0:T(8,128)}, f32[64,48,128]{2,1,0:T(8,128)S(1)}, u32[]{:S(2)}) copy-start(f32[64,48,128]{2,1,0:T(8,128)S(1)} %all-to-all-done.1.x_ref) | copy-start | bytes 4718596
  64.1 28.1 %all-to-all-start = ((f32[64,16,128]{2,1,0:T(8,128)}), f32[64,16,128]{2,1,0:T(8,128)S(1)}, u32[]{:S(2)}, u32[]{:S(2)}) async-start(f32[64,16,128]{2,1,0:T(8,128)} %bitcast.42), calls=%async_computation | async-start | bytes 1048576 | tf_op jit(solution)/shard_map/all_to_all | solution.py:285
  92.1 0.8 copy-start.1

commit v2 on v1

--- a/solution.py
+++ b/solution.py
@@ -166,7 +166,7 @@
     return ref.reshape(members * tiles, width).at[pl.ds(tile, members, stride=tiles), :]
 
 
-def analysis_kernel(col_ref, root_ref, value_ref, x_ref, out_ref, *, groups):
+def analysis_kernel(obs_ref, x_ref, out_ref, *, groups, row_of):
     members = x_ref.shape[0]
     spare = members - 1.0
     wide = GROUP * members
@@ -195,7 +195,8 @@
         averages, anomalies = [], []
         spread = jnp.zeros((members, LANE), jnp.float32)
         there = jnp.zeros((8, LANE), jnp.float32)
-        index = jnp.broadcast_to(col_ref[pl.ds(g, 1), :], (members, LANE))
+        row = pl.ds(row_of(g), 1)
+        index = jnp.broadcast_to(obs_ref[0, row, :].astype(jnp.int32), (members, LANE))
         for b in range(GROUP):
             x = tile_of(x_ref, g * GROUP + b)[...]
             average = jnp.mean(x, axis=0, keepdims=True)
@@ -208,9 +209,9 @@
                 jnp.broadcast_to(average, (8, LANE)), index[:8], axis=1, mode="promise_in_bounds"
             )
             there = jnp.where(slots_of[b], mean_seen, there)
-        root = root_ref[pl.ds(g, 1), :]
+        root = obs_ref[1, row, :]
         scaled = spread * root
-        innovation = root * (value_ref[pl.ds(g, 1), :] - there[:1])
+        innovation = root * (obs_ref[2, row, :] - there[:1])
         yield
         scaled_split = split(scaled)
         wanted = jnp.concatenate([innovation, spare_rows[:, :LANE]], axis=0)
@@ -258,27 +259,26 @@
         running = [r for r in running if next(r, running) is None]
 
 
-def analyse(background, observations, groups, total, first_block, earlier=None):
+def analyse(background, observations, groups, total, first_block, row_of, earlier=None):
     members, rows, width = background.shape
     tiles = groups * GROUP
-    packed = [a.reshape(rows // tiles, groups, LANE) for a in observations]
-    spec = pl.BlockSpec((None, groups, LANE), lambda i: (i, 0, 0))
     field = lambda shift: pl.BlockSpec((members, tiles, width), lambda i: (0, i + shift, 0))
-    kernel = functools.partial(analysis_kernel, groups=groups)
+    kernel = functools.partial(analysis_kernel, groups=groups, row_of=row_of)
     more = {}
     if earlier is not None:
         inner = kernel
-        kernel = lambda a, b, c, x, _, out: inner(a, b, c, x, out)
-        more = {"input_output_aliases": {4: 0}}
+        kernel = lambda o, x, _, out: inner(o, x, out)
+        more = {"input_output_aliases": {2: 0}}
     return pl.pallas_call(
         kernel,
         grid=(rows // tiles,),
         out_shape=jax.ShapeDtypeStruct((members, total, width), jnp.float32),
-        in_specs=[spec, spec, spec, field(0)] + [pl.BlockSpec(memory_space=pl.ANY)] * len(more),
+        in_specs=[pl.BlockSpec(observations.shape, lambda i: (0, 0, 0)), field(0)]
+        + [pl.BlockSpec(memory_space=pl.ANY)] * len(more),
         out_specs=field(first_block),
         name="analysis",
         **more,
-    )(*packed, background, *([] if earlier is None else [earlier]))
+    )(observations, background, *([] if earlier is None else [earlier]))
 
 
 def exchange(x):
@@ -293,29 +293,28 @@
     down = [(j, i) for i, j in up]
     edge = height // 8
     kept = height - 2 * edge
-    blocks = kept // (4 * GROUP)
-    inner = slice(edge, height - edge)
-    outer = lambda a, axis: jnp.concatenate(
-        [lax.slice_in_dim(a, 0, edge, axis=axis), lax.slice_in_dim(a, height - edge, height, axis=axis)],
-        axis=axis,
-    )
+    blocks = kept // (2 * edge)
+    before = edge // GROUP
+    groups = 2 * before
+    inner_row = lambda g: before + groups * pl.program_id(0) + g
+    outer_row = lambda g: g if g < before else height // GROUP - 2 * before + g
     columns = observed_column[:, 0]
     values = observed_value[:, 0]
     active = (jnp.arange(SLOTS, dtype=jnp.int32)[None, :] < slot_count).astype(jnp.float32)
     offset = (columns.astype(jnp.float32) - 0.5 * (COLS - 1)) / radius.astype(jnp.float32)
     root_weight = jnp.sqrt(active / (1.0 + offset * offset) / error_variance[:, 0])
-    inner_obs = [a[inner] for a in (columns, root_weight, values)]
-    outer_obs = [outer(a, 0) for a in (columns, root_weight, values)]
+    observations = jnp.stack([columns.astype(jnp.float32), root_weight, values])
+    observations = observations.reshape(3, height // GROUP, LANE)
     edges = jnp.stack([here == 0, here == devices - 1]).astype(jnp.int32)
 
+    above = lax.ppermute(jnp.concatenate([ensemble[:, -2:], velocity[:, -2:]], axis=0), "tile", up)
+    below = lax.ppermute(jnp.concatenate([ensemble[:, :2], velocity[:, :2]], axis=0), "tile", down)
     first = forecast_inner(ensemble, velocity, edge, kept)
     first = exchange(first.reshape(-1, kept, COLS))
-    above = lax.ppermute(jnp.concatenate([ensemble[:, -2:], velocity[:, -2:]], axis=0), "tile", up)
-    below = lax.ppermute(jnp.concatenate([ensemble[:, :2], velocity[:, :2]], axis=0), "tile", down)
     second = forecast_edge(edges, ensemble, velocity, above, below, edge)
     second = exchange(second.reshape(-1, 2 * edge, COLS))
-    done = analyse(first, inner_obs, 4, height, 0)
-    done = analyse(second, outer_obs, 4, height, blocks, done)
+    done = analyse(first, observations, groups, height, 0, inner_row)
+    done = analyse(second, observations, groups, height, blocks, outer_row, done)
     done = exchange(done)
     both = jnp.concatenate([done[:, kept : kept + edge], done[:, :kept], done[:, kept + edge :]], axis=1)
     both = both.reshape(-1, members, height, COLS)

time: 164 us -> 160 us (0.976)
  local copies, waits for them, and re-layouts: 9.35 us -> 5.3 us
  blocking collectives: 61 us -> 57.3 us
  waiting for transfers between devices: 31.5 us -> 35.2 us
    reshape x6 -> x0, local copies, waits for them, and re-layouts: 4.03 us -> none  [analyse(): packed = [a.reshape(rows // tiles, groups, LANE) for a in observations]]
    all_to_all x1, blocking collectives: 61 us -> 57.3 us  [exchange(): return lax.all_to_all(x, 'member', 0, 0, tiled=True)]
    all_to_all x2, waiting for transfers between devices: 0.01 us -> 3.68 us  [exchange(): return lax.all_to_all(x, 'member', 0, 0, tiled=True)]
  transfers between devices with their start and end apart: 4 -> 4, of which waited for: 2 -> 3; matrix products, arithmetic and copies ran while one was open for 4% -> 2% of each run, Pallas kernels for 11% -> 12%
where the time goes in v2:
time: 160 us; the launch traced here: 158 us
  blocking collectives  57.3 us (36%)
  waiting for transfers between devices  35.2 us (22%)
  Pallas kernels  30.4 us (19%)
  starting transfers between devices  27.7 us (17%)
  local copies, waits for them, and re-layouts  5.3 us (3%)
  other arithmetic  1.61 us (1%)
    all_to_all x1, blocking collectives, exchange(): return lax.all_to_all(x, 'member', 0, 0, tiled=True)  57.3 us
    ppermute x1, waiting for transfers between devices, per_device(): lax.ppermute(jnp.concatenate([ensemble[:, -2:], velocity[:, -2:]], axis=0...  30.4 us
    all_to_all x2, starting transfers between devices, exchange(): return lax.all_to_all(x, 'member', 0, 0, tiled=True)  21.6 us
    pallas_call x2, Pallas kernels, analyse(): pl.pallas_call(kernel, grid=(rows // tiles,), out_shape=jax.ShapeDtypeStr...  18.8 us
    pallas_call x1, Pallas kernels, forecast_inner(): pl.pallas_call(functools.partial(inner_kernel, row0=row0, kept=kept), gri...  6.35 us
    pallas_call x1, Pallas kernels, forecast_edge(): pl.pallas_call(functools.partial(edge_kernel, kept=kept), grid=(width //...  5.28 us
    all_to_all x2, waiting for transfers between devices, exchange(): return lax.all_to_all(x, 'member', 0, 0, tiled=True)  3.68 us
    ppermute x1, starting transfers between devices, per_device(): lax.ppermute(jnp.concatenate([ensemble[:, :2], velocity[:, :2]], axis=0),...  3.53 us
  transfers between devices with their start and end apart: 4, of which 3 were waited for; matrix products, arithmetic and copies ran while one was open for 2% of the time, Pallas kernels for 12%

profile of v2, /device:TPU:7, one launch (start us, length us, event | category | flops | bytes accessed | tf_op | source)
XLA Modules:
  0.0 157.7 jit_solution(2738808292345299726)
XLA Ops:
  0.0 6.4 %forecast_inner.1 = f32[32,2,48,128]{3,2,1,0:T(8,128)} custom-call(f32[2,64,4096]{2,1,0:T(8,128)} %refs_2_.3, f32[2,64,4096]{2,1,0:T(8,128)} %refs_2_.3, f32[2,64,4096]{2,1,0:T(8,128)} %refs_2_.3, f32[2,64,4096]{2,1,0:T(8,128)} %refs_5_.3, f32[2,64,4096]{2,1,0:T(8,128)} %refs_5_.3, f32[2,64,4096]{2,1,0:T(8,128)} %refs_5_.3), custom_call_target="tpu_custom_call" | custom-call | tf_op jit(solution)/shard_map/forecast_inner/pallas_call | solution.py:110
  6.4 11.9 %all-to-all-start.1 = ((f32[64,48,128]{2,1,0:T(8,128)}), f32[64,48,128]{2,1,0:T(8,128)S(1)}, u32[]{:S(2)}, u32[]{:S(2)}) async-start(f32[64,48,128]{2,1,0:T(8,128)} %bitcast.25), calls=%async_computation.1 | async-start | bytes 3145728 | tf_op jit(solution)/shard_map/all_to_all | solution.py:285
  18.3 1.3 fusion.1
  19.6 2.6 %collective-permute-start = (f32[4,2,4096]{2,1,0:T(2,128)S(1)}, f32[4,2,4096]{2,1,0:T(2,128)S(1)}, u32[]{:S(2)}, u32[]{:S(2)}) collective-permute-start(f32[4,2,4096]{2,1,0:T(2,128)S(1)} %pad_maximum_fusion.1), channel_id=1, source_target_pairs={{0,1},{1,2},{2,3},{3,4},{4,5},{5,6},{6,7},{8,9},{9,10},{10,11},{11... | collective-permute-start | bytes 393224 | tf_op jit(solution)/shard_map/ppermute | solution.py:310
  22.4 3.5 %collective-permute-start.1 = (f32[4,2,4096]{2,1,0:T(2,128)S(1)}, f32[4,2,4096]{2,1,0:T(2,128)S(1)}, u32[]{:S(2)}, u32[]{:S(2)}) collective-permute-start(f32[4,2,4096]{2,1,0:T(2,128)S(1)} %pad_maximum_fusion.2), channel_id=1, source_target_pairs={{1,0},{2,1},{3,2},{4,3},{5,4},{6,5},{7,6},{9,8},{10,9},{11,10},{12... | collective-permute-start | bytes 393224 | tf_op jit(solution)/shard_map/ppermute | solution.py:311
  25.9 0.6 add_convert_fusion.edge_ref
  26.5 30.4 %collective-permute-done.refs_6_.refs_7_.refs_8_ = f32[4,2,4096]{2,1,0:T(2,128)S(1)} collective-permute-done((f32[4,2,4096]{2,1,0:T(2,128)S(1)}, f32[4,2,4096]{2,1,0:T(2,128)S(1)}, u32[]{:S(2)}, u32[]{:S(2)}) %collective-permute-start) | collective-permute-done | bytes 131104 | tf_op jit(solution)/shard_map/ppermute | solution.py:310
  56.9 1.1 collective-permute-done.1.refs_9_.refs_10_.refs_11_
  58.0 0.6 copy-done.3
  58.6 5.3 %forecast_edge.1 = f32[32,2,16,128]{3,2,1,0:T(8,128)} custom-call(s32[2]{0:T(128)} %add_convert_fusion.edge_ref, f32[2,64,4096]{2,1,0:T(8,128)} %refs_2_.3, f32[2,64,4096]{2,1,0:T(8,128)} %refs_2_.3, f32[2,64,4096]{2,1,0:T(8,128)} %refs_2_.3, f32[2,64,4096]{2,1,0:T(8,128)} %refs_5_.3, f32[2,64,4096]{2,1,0:T(8,128)} %refs_5_.3, f32[2,64,4096]{2,1,0:T(8,128)} %refs_5_.3, ...), custom_call_target="tpu_custom_call" | custom-call | tf_op jit(solution)/shard_map/forecast_edge/pallas_call | solution.py:123
  64.0 9.6 %all-to-all-start = ((f32[64,16,128]{2,1,0:T(8,128)}), f32[64,16,128]{2,1,0:T(8,128)S(1)}, u32[]{:S(2)}, u32[]{:S(2)}) async-start(f32[64,16,128]{2,1,0:T(8,128)} %bitcast.26), calls=%async_computation | async-start | bytes 1048576 | tf_op jit(solution)/shard_map/all_to_all | solution.py:285
  73.6 0.1 lt.28
  73.7 0.1 copy.13
  74.2 0.1 copy.15
  74.3 0.1 copy.14
  74.5 0.6 pad_maximum_fusion.3.obs_ref.o
  75.2 13.2 %analysis.2._ = f32[64,64,128]{2,1,0:T(8,128)} custom-call(f32[3,16,128]{2,1,0:T(8,128)} %pad_maximum_fusion.3.obs_ref.o, f32[64,48,128]{2,1,0:T(8,128)} %copy-done), custom_call_target="tpu_custom_call" | custom-call | tf_op jit(solution)/shard_map/analysis/pallas_call | solution.py:272
  88.3 3.7 %all-to-all-done.x = f32[64,16,128]{2,1,0:T(8,128)S(1)} async-done(((f32[64,16,128]{2,1,0:T(8,128)}), f32[64,16,128]{2,1,0:T(8,128)S(1)}, u32[]{:S(2)}, u32[]{:S(2)}) %all-to-all-start) | async-done | bytes 524320 | tf_op jit(solution)/shard_map/all_to_all | solution.py:285
  92.0 0.8 copy-done.1
  92.8 5.6 %analysis.3 = f32[64,64,128]{2,1,0:T(8,128)} custom-call(f32[3,16,128]{2,1,0:T(8,128)} %pad_maximum_fusion.3.obs_ref.o, f32[64,16,128]{2,1,0:T(8,128)} %copy-done.1, f32[64,64,128]{2,1,0:T(8,128)} %analysis.2._), custom_call_target="tpu_custom_call", output_to_operand_aliasing={{}: (2, {})} | custom-call | tf_op jit(solution)/shard_map/analysis/pallas_call | solution.py:272
  98.4 57.3 %all_to_all.15 = f32[64,64,128]{2,1,0:T(8,128)S(1)} all-to-all(f32[64,64,128]{2,1,0:T(8,128)} %analysis.3), channel_id=1, replica_groups=mesh['member'=32,'tile'=8] {'member'}, dimensions={0} | all-to-all | bytes 4194304 | tf_op jit(solution)/shard_map/all_to_all | solution.py:285
  155.8 0.1 slice.29
  155.9 0.3 pad_maximum_fusion
  156.2 1.5 copy.19
  (31 shorter events, 0.8 us)
Async XLA Ops:
  6.4 57.6 %all-to-all-start.1 = ((f32[64,48,128]{2,1,0:T(8,128)}), f32[64,48,128]{2,1,0:T(8,128)S(1)}, u32[]{:S(2)}, u32[]{:S(2)}) async-start(f32[64,48,128]{2,1,0:T(8,128)} %bitcast.25), calls=%async_computation.1 | async-start | bytes 3145728 | tf_op jit(solution)/shard_map/all_to_all | solution.py:285
  19.6 37.3 %collective-permute-start = (f32[4,2,4096]{2,1,0:T(2,128)S(1)}, f32[4,2,4096]{2,1,0:T(2,128)S(1)}, u32[]{:S(2)}, u32[]{:S(2)}) collective-permute-start(f32[4,2,4096]{2,1,0:T(2,128)S(1)} %pad_maximum_fusion.1), channel_id=1, source_target_pairs={{0,1},{1,2},{2,3},{3,4},{4,5},{5,6},{6,7},{8,9},{9,10},{10,11},{11... | collective-permute-start | bytes 393224 | tf_op jit(solution)/shard_map/ppermute | solution.py:310
  22.4 35.6 %collective-permute-start.1 = (f32[4,2,4096]{2,1,0:T(2,128)S(1)}, f32[4,2,4096]{2,1,0:T(2,128)S(1)}, u32[]{:S(2)}, u32[]{:S(2)}) collective-permute-start(f32[4,2,4096]{2,1,0:T(2,128)S(1)} %pad_maximum_fusion.2), channel_id=1, source_target_pairs={{1,0},{2,1},{3,2},{4,3},{5,4},{6,5},{7,6},{9,8},{10,9},{11,10},{12... | collective-permute-start | bytes 393224 | tf_op jit(solution)/shard_map/ppermute | solution.py:311
  26.5 47.2 %copy-start.6 = (s32[64,1,32]{0,2,1:T(8,128)S(1)}, s32[64,1,32]{0,2,1:T(8,128)}, u32[]{:S(2)}) copy-start(s32[64,1,32]{0,2,1:T(8,128)} %param.9) | copy-start | bytes 24580
  26.5 47.4 %copy-start.8 = (s32[64,1]{0,1:T(1,128)S(1)}, s32[64,1]{0,1:T(1,128)}, u32[]{:S(2)}) copy-start(s32[64,1]{0,1:T(1,128)} %param.11) | copy-start | bytes 772
  26.5 47.5 %copy-start.7 = (s32[64,1]{0,1:T(1,128)S(1)}, s32[64,1]{0,1:T(1,128)}, u32[]{:S(2)}) copy-start(s32[64,1]{0,1:T(1,128)} %param.10) | copy-start | bytes 772
  26.5 47.7 %copy-start.4 = (f32[64,1,32]{0,2,1:T(8,128)S(1)}, f32[64,1,32]{0,2,1:T(8,128)}, u32[]{:S(2)}) copy-start(f32[64,1,32]{0,2,1:T(8,128)} %param.12) | copy-start | bytes 24580
  26.5 47.8 %copy-start.5 = (f32[64,1,32]{0,2,1:T(8,128)S(1)}, f32[64,1,32]{0,2,1:T(8,128)}, u32[]{:S(2)}) copy-start(f32[64,1,32]{0,2,1:T(8,128)} %param.13) | copy-start | bytes 24580
  56.9 1.1 copy-start.2
  58.0 0.6 copy-start.3
  63.9 11.2 %copy-start = (f32[64,48,128]{2,1,0:T(8,128)}, f32[64,48,128]{2,1,0:T(8,128)S(1)}, u32[]{:S(2)}) copy-start(f32[64,48,128]{2,1,0:T(8,128)S(1)} %all-to-all-done.1.x_ref) | copy-start | bytes 4718596
  64.0 28.1 %all-to-all-start = ((f32[64,16,128]{2,1,0:T(8,128)}), f32[64,16,128]{2,1,0:T(8,128)S(1)}, u32[]{:S(2)}, u32[]{:S(2)}) async-start(f32[64,16,128]{2,1,0:T(8,128)} %bitcast.26), calls=%async_computation | async-start | bytes 1048576 | tf_op jit(solution)/shard_map/all_to_all | solution.py:285
  92.0 0.8 copy-start.1

commit v3 on v2

--- a/solution.py
+++ b/solution.py
@@ -79,28 +79,32 @@
 
 
 def edge_kernel(edge_ref, *refs, kept):
-    *refs, out_ref = refs
-    height = refs[0].shape[1]
+    *refs, _, out_ref = refs
+    tall = refs[0].shape[1]
     far = jnp.zeros((SIDE - 2, out_ref.shape[0] * LANE + 2 * LANE), jnp.float32)
-    body = lambda i, rows: joined(refs[3 * (i // 2) : 3 * (i // 2) + 3], i % 2, rows)
-    beyond = lambda j, i: joined(refs[6 + 3 * j : 9 + 3 * j], i, slice(None))
+    body = lambda first, i, rows: joined(refs[first + 3 * (i // 2) : first + 3 * (i // 2) + 3], i % 2, rows)
+    beyond = lambda j, i: joined(refs[12 + 3 * j : 15 + 3 * j], i, slice(None))
     top = [
-        jnp.concatenate([far, beyond(0, i), body(i, slice(0, kept + SIDE))], axis=0) for i in range(4)
+        jnp.concatenate([far, beyond(0, i), body(0, i, slice(0, kept + SIDE))], axis=0) for i in range(4)
     ]
     advance(top, out_ref, 0, jnp.where(edge_ref[0] == 1, SIDE, -1), None)
     bottom = [
-        jnp.concatenate([body(i, slice(height - kept - SIDE, height)), beyond(1, i), far], axis=0)
+        jnp.concatenate([body(6, i, slice(tall - kept - SIDE, tall)), beyond(1, i), far], axis=0)
         for i in range(4)
     ]
     advance(bottom, out_ref, kept, None, jnp.where(edge_ref[1] == 1, SIDE + kept - 1, -1))
 
 
-def around(count, height, width):
+def vmem():
+    return pl.BlockSpec(memory_space=pltpu.VMEM)
+
+
+def around(count, height, width, row=0):
     per, last = BLOCK // LANE, width // LANE - 1
     return [
-        pl.BlockSpec((count, height, LANE), lambda k: (0, 0, jnp.maximum(per * k - 1, 0))),
-        pl.BlockSpec((count, height, BLOCK), lambda k: (0, 0, k)),
-        pl.BlockSpec((count, height, LANE), lambda k: (0, 0, jnp.minimum(per * (k + 1), last))),
+        pl.BlockSpec((count, height, LANE), lambda k: (0, row, jnp.maximum(per * k - 1, 0))),
+        pl.BlockSpec((count, height, BLOCK), lambda k: (0, row, k)),
+        pl.BlockSpec((count, height, LANE), lambda k: (0, row, jnp.minimum(per * (k + 1), last))),
     ]
 
 
@@ -110,27 +114,31 @@
     return pl.pallas_call(
         functools.partial(inner_kernel, row0=row0, kept=kept),
         grid=(width // BLOCK,),
-        out_shape=jax.ShapeDtypeStruct((width // COLS, members, kept, COLS), jnp.float32),
+        out_shape=jax.ShapeDtypeStruct((width // COLS, members, height, COLS), jnp.float32),
         in_specs=around(members, height, width) + around(2, height, width),
         out_specs=pl.BlockSpec((per, members, kept, COLS), lambda k: (k, 0, 0, 0)),
         name="forecast_inner",
     )(*[ensemble] * 3, *[velocity] * 3)
 
 
-def forecast_edge(edges, ensemble, velocity, above, below, kept):
+def forecast_edge(edges, ensemble, velocity, above, below, kept, partial):
     members, height, width = ensemble.shape
     per = BLOCK // LANE
+    tall = kept + SIDE
+    both = lambda row: around(members, tall, width, row) + around(2, tall, width, row)
     return pl.pallas_call(
         functools.partial(edge_kernel, kept=kept),
         grid=(width // BLOCK,),
-        out_shape=jax.ShapeDtypeStruct((width // COLS, members, 2 * kept, COLS), jnp.float32),
+        out_shape=jax.ShapeDtypeStruct(partial.shape, jnp.float32),
         in_specs=[pl.BlockSpec(memory_space=pltpu.SMEM)]
-        + around(members, height, width)
-        + around(2, height, width)
-        + around(4, 2, width) * 2,
-        out_specs=pl.BlockSpec((per, members, 2 * kept, COLS), lambda k: (k, 0, 0, 0)),
+        + both(0)
+        + both(height // tall - 1)
+        + around(4, 2, width) * 2
+        + [pl.BlockSpec(memory_space=pl.ANY)],
+        out_specs=pl.BlockSpec((per, members, 2 * kept, COLS), lambda k: (k, 0, height // (2 * kept) - 1, 0)),
+        input_output_aliases={19: 0},
         name="forecast_edge",
-    )(edges, *[ensemble] * 3, *[velocity] * 3, *[above] * 3, *[below] * 3)
+    )(edges, *([ensemble] * 3 + [velocity] * 3) * 2, *[above] * 3, *[below] * 3, partial)
 
 
 def split(x, parts=2):
@@ -187,6 +195,10 @@
         0.0,
     )
     spare_rows = jnp.zeros((15, wide), jnp.float32)
+    per = LANE // members
+    first_half = lax.broadcasted_iota(jnp.int32, (members, LANE), 1) < members
+    first_half16 = jnp.where(first_half, 1.0, 0.0).astype(jnp.bfloat16)
+    base = pl.program_id(0) * (groups * GROUP)
 
     def stacked(parts, mask):
         return [jnp.concatenate([part] * GROUP, axis=0) * mask for part in parts]
@@ -198,7 +210,7 @@
         row = pl.ds(row_of(g), 1)
         index = jnp.broadcast_to(obs_ref[0, row, :].astype(jnp.int32), (members, LANE))
         for b in range(GROUP):
-            x = tile_of(x_ref, g * GROUP + b)[...]
+            x = tile_of(x_ref, base + g * GROUP + b)[...]
             average = jnp.mean(x, axis=0, keepdims=True)
             anomaly = x - average
             averages.append(average)
@@ -233,25 +245,34 @@
             right = stacked(split(factor), block)
             last = number == SWEEPS - 1
             if last:
-                stage = times(jnp.concatenate([result, wanted], axis=0), right)
-                result, wanted = stage[:members], stage[members:]
+                result = times(result, right)
             elif number == 0:
-                stage = times(jnp.concatenate([system, wanted], axis=0), right)
-                result, wanted = factor, stage[members:]
+                stage, result = times(system, right), factor
             else:
-                stage = times(jnp.concatenate([system, result, wanted], axis=0), right)
-                result, wanted = stage[members : 2 * members], stage[2 * members :]
+                stage = times(jnp.concatenate([system, result], axis=0), right)
+                result = stage[members:]
             yield
             if not last:
                 system = times(stage[:members], right)
                 yield
-        mean_weight = times(wanted, stacked(split(result), block))[:1] * inverse
-        yield
-        gain = split((spare**0.5 * root_norm) * result + mean_weight)
-        high, low = split(jnp.concatenate(anomalies, axis=0))
-        part = product(stacked(gain, block), [high, low])
+        right = stacked(split(result), block)
+        wanted = times(wanted, right)
+        yield
+        mean_weight = times(wanted, right)[:1] * inverse
+        yield
+        high, low = split((spare**0.5 * root_norm) * result + mean_weight)
         for b in range(GROUP):
-            tile_of(out_ref, g * GROUP + b)[...] = part[members * b : members * (b + 1)] + averages[b]
+            at = LANE * (b // per)
+            here, there_low = high[:, at : at + LANE], low[:, at : at + LANE]
+            turned = lambda part: pltpu.roll(part.astype(jnp.float32), members, 1).astype(jnp.bfloat16)
+            if b % per:
+                left = jnp.where(first_half, turned(here), there_low)
+            else:
+                left = jnp.where(first_half, here, turned(there_low))
+            left = jnp.concatenate([left, left * first_half16], axis=1)
+            a_high, a_low = split(anomalies[b])
+            right = jnp.concatenate([a_high, a_high, a_low, jnp.zeros_like(a_low)], axis=0)
+            tile_of(out_ref, base + g * GROUP + b)[...] = mm(left, right) + averages[b]
         yield
 
     running = [one(g) for g in range(groups)]
@@ -259,26 +280,17 @@
         running = [r for r in running if next(r, running) is None]
 
 
-def analyse(background, observations, groups, total, first_block, row_of, earlier=None):
-    members, rows, width = background.shape
-    tiles = groups * GROUP
-    field = lambda shift: pl.BlockSpec((members, tiles, width), lambda i: (0, i + shift, 0))
-    kernel = functools.partial(analysis_kernel, groups=groups, row_of=row_of)
-    more = {}
-    if earlier is not None:
-        inner = kernel
-        kernel = lambda o, x, _, out: inner(o, x, out)
-        more = {"input_output_aliases": {2: 0}}
+def analyse(background, observations, groups, row_of):
+    _, rows, _ = background.shape
     return pl.pallas_call(
-        kernel,
-        grid=(rows // tiles,),
-        out_shape=jax.ShapeDtypeStruct((members, total, width), jnp.float32),
-        in_specs=[pl.BlockSpec(observations.shape, lambda i: (0, 0, 0)), field(0)]
-        + [pl.BlockSpec(memory_space=pl.ANY)] * len(more),
-        out_specs=field(first_block),
+        functools.partial(analysis_kernel, groups=groups, row_of=row_of),
+        grid=(rows // (groups * GROUP),),
+        out_shape=pltpu.VMEM(background.shape, jnp.float32),
+        in_specs=[vmem(), vmem()],
+        out_specs=vmem(),
+        compiler_params=pltpu.CompilerParams(vmem_limit_bytes=32 << 20),
         name="analysis",
-        **more,
-    )(observations, background, *([] if earlier is None else [earlier]))
+    )(observations, pltpu.with_memory_space_constraint(background, pltpu.VMEM))
 
 
 def exchange(x):
@@ -293,11 +305,14 @@
     down = [(j, i) for i, j in up]
     edge = height // 8
     kept = height - 2 * edge
-    blocks = kept // (2 * edge)
-    before = edge // GROUP
-    groups = 2 * before
-    inner_row = lambda g: before + groups * pl.program_id(0) + g
-    outer_row = lambda g: g if g < before else height // GROUP - 2 * before + g
+    groups = 2 * edge // GROUP
+    inner_steps = kept // (2 * edge)
+
+    def row_of(g):
+        step, half = pl.program_id(0), groups // 2
+        outer = g if g < half else height // GROUP - groups + g
+        return jnp.where(step < inner_steps, half + groups * step + g, outer)
+
     columns = observed_column[:, 0]
     values = observed_value[:, 0]
     active = (jnp.arange(SLOTS, dtype=jnp.int32)[None, :] < slot_count).astype(jnp.float32)
@@ -309,12 +324,10 @@
 
     above = lax.ppermute(jnp.concatenate([ensemble[:, -2:], velocity[:, -2:]], axis=0), "tile", up)
     below = lax.ppermute(jnp.concatenate([ensemble[:, :2], velocity[:, :2]], axis=0), "tile", down)
-    first = forecast_inner(ensemble, velocity, edge, kept)
-    first = exchange(first.reshape(-1, kept, COLS))
-    second = forecast_edge(edges, ensemble, velocity, above, below, edge)
-    second = exchange(second.reshape(-1, 2 * edge, COLS))
-    done = analyse(first, observations, groups, height, 0, inner_row)
-    done = analyse(second, observations, groups, height, blocks, outer_row, done)
+    fields = forecast_inner(ensemble, velocity, edge, kept)
+    fields = forecast_edge(edges, ensemble, velocity, above, below, edge, fields)
+    fields = exchange(fields.reshape(-1, height, COLS))
+    done = analyse(fields, observations, groups, row_of)
     done = exchange(done)
     both = jnp.concatenate([done[:, kept : kept + edge], done[:, :kept], done[:, kept + edge :]], axis=1)
     both = both.reshape(-1, members, height, COLS)

time: 160 us -> 157 us (0.981)
  waiting for transfers between devices: 35.2 us -> 49.5 us
  starting transfers between devices: 27.7 us -> 17.9 us
  blocking collectives: 57.3 us -> 54 us
  Pallas kernels: 30.4 us -> 27.7 us
    all_to_all x2 -> x1, waiting for transfers between devices: 3.68 us -> 49.5 us  [exchange(): return lax.all_to_all(x, 'member', 0, 0, tiled=True)]
    ppermute x1, waiting for transfers between devices: 30.4 us -> 0.01 us  [per_device(): lax.ppermute(jnp.concatenate([ensemble[:, -2:], velocity[:, -2:]], axis=0...]
    all_to_all x2 -> x1, starting transfers between devices: 21.6 us -> 12.2 us  [exchange(): return lax.all_to_all(x, 'member', 0, 0, tiled=True)]
    all_to_all x1, blocking collectives: 57.3 us -> 54 us  [exchange(): return lax.all_to_all(x, 'member', 0, 0, tiled=True)]
    pallas_call x2 -> x1, Pallas kernels: 18.8 us -> 16.4 us  [analyse(): pl.pallas_call(functools.partial(analysis_kernel, groups=groups, row_of=r...]
  transfers between devices with their start and end apart: 4 -> 3, of which waited for: 3 -> 1; matrix products, arithmetic and copies ran while one was open for 2% -> 1% of each run, Pallas kernels for 12% -> 4%
where the time goes in v3:
time: 157 us; the launch traced here: 155 us
  blocking collectives  54 us (34%)
  waiting for transfers between devices  49.5 us (32%)
  Pallas kernels  27.7 us (18%)
  starting transfers between devices  17.9 us (11%)
  local copies, waits for them, and re-layouts  5.16 us (3%)
    all_to_all x1, blocking collectives, exchange(): return lax.all_to_all(x, 'member', 0, 0, tiled=True)  54 us
    all_to_all x1, waiting for transfers between devices, exchange(): return lax.all_to_all(x, 'member', 0, 0, tiled=True)  49.5 us
    pallas_call x1, Pallas kernels, analyse(): pl.pallas_call(functools.partial(analysis_kernel, groups=groups, row_of=r...  16.4 us
    all_to_all x1, starting transfers between devices, exchange(): return lax.all_to_all(x, 'member', 0, 0, tiled=True)  12.2 us
    pallas_call x1, Pallas kernels, forecast_inner(): pl.pallas_call(functools.partial(inner_kernel, row0=row0, kept=kept), gri...  6.37 us
    pallas_call x1, Pallas kernels, forecast_edge(): pl.pallas_call(functools.partial(edge_kernel, kept=kept), grid=(width //...  4.89 us
    ppermute x1, starting transfers between devices, per_device(): lax.ppermute(jnp.concatenate([ensemble[:, :2], velocity[:, :2]], axis=0),...  3.81 us
  transfers between devices with their start and end apart: 3, of which 1 were waited for; matrix products, arithmetic and copies ran while one was open for 1% of the time, Pallas kernels for 4%

profile of v3, /device:TPU:7, one launch (start us, length us, event | category | flops | bytes accessed | tf_op | source)
XLA Modules:
  0.0 155.5 jit_solution(7566000287301675170)
XLA Ops:
  0.0 1.3 fusion.1
  1.4 3.8 %collective-permute-start.1 = (f32[4,2,4096]{2,1,0:T(2,128)S(1)}, f32[4,2,4096]{2,1,0:T(2,128)S(1)}, u32[]{:S(2)}, u32[]{:S(2)}) collective-permute-start(f32[4,2,4096]{2,1,0:T(2,128)S(1)} %pad_maximum_fusion.2), channel_id=1, source_target_pairs={{1,0},{2,1},{3,2},{4,3},{5,4},{6,5},{7,6},{9,8},{10,9},{11,10},{12... | collective-permute-start | bytes 393224 | tf_op jit(solution)/shard_map/ppermute | solution.py:326
  5.2 1.9 %collective-permute-start = (f32[4,2,4096]{2,1,0:T(2,128)S(1)}, f32[4,2,4096]{2,1,0:T(2,128)S(1)}, u32[]{:S(2)}, u32[]{:S(2)}) collective-permute-start(f32[4,2,4096]{2,1,0:T(2,128)S(1)} %pad_maximum_fusion.1), channel_id=1, source_target_pairs={{0,1},{1,2},{2,3},{3,4},{4,5},{5,6},{6,7},{8,9},{9,10},{10,11},{11... | collective-permute-start | bytes 393224 | tf_op jit(solution)/shard_map/ppermute | solution.py:325
  7.2 6.4 %forecast_inner.1.refs_18_ = f32[32,2,64,128]{3,2,1,0:T(8,128)} custom-call(f32[2,64,4096]{2,1,0:T(8,128)} %refs_8_.1, f32[2,64,4096]{2,1,0:T(8,128)} %refs_8_.1, f32[2,64,4096]{2,1,0:T(8,128)} %refs_8_.1, f32[2,64,4096]{2,1,0:T(8,128)} %refs_11_.1, f32[2,64,4096]{2,1,0:T(8,128)} %refs_11_.1, f32[2,64,4096]{2,1,0:T(8,128)} %refs_11_.1), custom_call_target="tpu_custom_call" | custom-call | tf_op jit(solution)/shard_map/forecast_inner/pallas_call | solution.py:114
  13.5 0.7 add_convert_fusion.edge_ref
  14.2 0.6 copy-done
  14.9 0.6 copy-done.1
  15.5 4.9 %forecast_edge.1 = f32[32,2,64,128]{3,2,1,0:T(8,128)} custom-call(s32[2]{0:T(128)} %add_convert_fusion.edge_ref, f32[2,64,4096]{2,1,0:T(8,128)} %refs_8_.1, f32[2,64,4096]{2,1,0:T(8,128)} %refs_8_.1, f32[2,64,4096]{2,1,0:T(8,128)} %refs_8_.1, f32[2,64,4096]{2,1,0:T(8,128)} %refs_11_.1, f32[2,64,4096]{2,1,0:T(8,128)} %refs_11_.1, ...), custom_call_target="tpu_custom_call", output_to_operand_aliasing={{}: (19, {})} | custom-call | tf_op jit(solution)/shard_map/forecast_edge/pallas_call | solution.py:129
  20.5 12.2 %all-to-all-start = ((f32[64,64,128]{2,1,0:T(8,128)}), f32[64,64,128]{2,1,0:T(8,128)S(1)}, u32[]{:S(2)}, u32[]{:S(2)}) async-start(f32[64,64,128]{2,1,0:T(8,128)} %bitcast.23), calls=%async_computation | async-start | bytes 4194304 | tf_op jit(solution)/shard_map/all_to_all | solution.py:297
  32.7 0.1 copy.13
  32.8 0.1 convert_element_type.40
  32.9 0.1 div.31
  33.0 0.1 lt.30
  33.1 0.1 copy.14
  33.2 0.1 squeeze.4
  33.3 0.1 lt.28
  33.4 0.1 copy.15
  33.5 0.1 stack.16
  33.6 49.5 %all-to-all-done.x_ref = f32[64,64,128]{2,1,0:T(8,128)S(1)} async-done(((f32[64,64,128]{2,1,0:T(8,128)}), f32[64,64,128]{2,1,0:T(8,128)S(1)}, u32[]{:S(2)}, u32[]{:S(2)}) %all-to-all-start) | async-done | bytes 2097184 | tf_op jit(solution)/shard_map/all_to_all | solution.py:297
  83.1 16.4 %analysis.1 = f32[64,64,128]{2,1,0:T(8,128)S(1)} custom-call(f32[3,16,128]{2,1,0:T(8,128)S(1)} %pad_maximum_fusion.3.obs_ref, f32[64,64,128]{2,1,0:T(8,128)S(1)} %all-to-all-done.x_ref), custom_call_target="tpu_custom_call" | custom-call | tf_op jit(solution)/shard_map/analysis/pallas_call | solution.py:285
  99.6 54.0 %all_to_all.10 = f32[64,64,128]{2,1,0:T(8,128)S(1)} all-to-all(f32[64,64,128]{2,1,0:T(8,128)S(1)} %analysis.1), channel_id=1, replica_groups=mesh['member'=32,'tile'=8] {'member'}, dimensions={0} | all-to-all | bytes 4194304 | tf_op jit(solution)/shard_map/all_to_all | solution.py:297
  153.6 0.1 slice.29
  153.7 0.3 pad_maximum_fusion
  153.9 1.5 copy.19
  (24 shorter events, 0.4 us)
Async XLA Ops:
  1.4 12.9 %collective-permute-start.1 = (f32[4,2,4096]{2,1,0:T(2,128)S(1)}, f32[4,2,4096]{2,1,0:T(2,128)S(1)}, u32[]{:S(2)}, u32[]{:S(2)}) collective-permute-start(f32[4,2,4096]{2,1,0:T(2,128)S(1)} %pad_maximum_fusion.2), channel_id=1, source_target_pairs={{1,0},{2,1},{3,2},{4,3},{5,4},{6,5},{7,6},{9,8},{10,9},{11,10},{12... | collective-permute-start | bytes 393224 | tf_op jit(solution)/shard_map/ppermute | solution.py:326
  5.2 9.0 %collective-permute-start = (f32[4,2,4096]{2,1,0:T(2,128)S(1)}, f32[4,2,4096]{2,1,0:T(2,128)S(1)}, u32[]{:S(2)}, u32[]{:S(2)}) collective-permute-start(f32[4,2,4096]{2,1,0:T(2,128)S(1)} %pad_maximum_fusion.1), channel_id=1, source_target_pairs={{0,1},{1,2},{2,3},{3,4},{4,5},{5,6},{6,7},{8,9},{9,10},{10,11},{11... | collective-permute-start | bytes 393224 | tf_op jit(solution)/shard_map/ppermute | solution.py:325
  14.2 0.6 copy-start
  14.9 0.6 copy-start.1
  20.4 12.3 %copy-start.4 = (s32[64,1,32]{0,2,1:T(8,128)S(1)}, s32[64,1,32]{0,2,1:T(8,128)}, u32[]{:S(2)}) copy-start(s32[64,1,32]{0,2,1:T(8,128)} %param.9) | copy-start | bytes 24580
  20.4 12.4 %copy-start.6 = (s32[64,1]{0,1:T(1,128)S(1)}, s32[64,1]{0,1:T(1,128)}, u32[]{:S(2)}) copy-start(s32[64,1]{0,1:T(1,128)} %param.11) | copy-start | bytes 772
  20.4 12.6 %copy-start.5 = (s32[64,1]{0,1:T(1,128)S(1)}, s32[64,1]{0,1:T(1,128)}, u32[]{:S(2)}) copy-start(s32[64,1]{0,1:T(1,128)} %param.10) | copy-start | bytes 772
  20.4 12.7 %copy-start.2 = (f32[64,1,32]{0,2,1:T(8,128)S(1)}, f32[64,1,32]{0,2,1:T(8,128)}, u32[]{:S(2)}) copy-start(f32[64,1,32]{0,2,1:T(8,128)} %param.13) | copy-start | bytes 24580
  20.5 12.9 %copy-start.3 = (f32[64,1,32]{0,2,1:T(8,128)S(1)}, f32[64,1,32]{0,2,1:T(8,128)}, u32[]{:S(2)}) copy-start(f32[64,1,32]{0,2,1:T(8,128)} %param.12) | copy-start | bytes 24580
  20.5 62.7 %all-to-all-start = ((f32[64,64,128]{2,1,0:T(8,128)}), f32[64,64,128]{2,1,0:T(8,128)S(1)}, u32[]{:S(2)}, u32[]{:S(2)}) async-start(f32[64,64,128]{2,1,0:T(8,128)} %bitcast.23), calls=%async_computation | async-start | bytes 4194304 | tf_op jit(solution)/shard_map/all_to_all | solution.py:297

commit v4 on v3

--- a/solution.py
+++ b/solution.py
@@ -73,23 +73,37 @@
 
 
 def inner_kernel(*refs, row0, kept):
-    *refs, out_ref = refs
+    *refs, out_ref, up_ref, down_ref = refs
     rows = slice(row0 - SIDE, row0 + kept + SIDE)
+    for i in range(4):
+        middle = refs[3 * (i // 2) + 1]
+        height = middle.shape[1]
+        up_ref[i] = middle[i % 2, height - 2 : height, :]
+        down_ref[i] = middle[i % 2, 0:2, :]
     advance([joined(refs[3 * (i // 2) : 3 * (i // 2) + 3], i % 2, rows) for i in range(4)], out_ref, 0, None, None)
 
 
 def edge_kernel(edge_ref, *refs, kept):
-    *refs, _, out_ref = refs
-    tall = refs[0].shape[1]
-    far = jnp.zeros((SIDE - 2, out_ref.shape[0] * LANE + 2 * LANE), jnp.float32)
+    *refs, above_ref, below_ref, out_ref = refs
+    tall, lanes = refs[0].shape[1], out_ref.shape[0] * LANE
+    far = jnp.zeros((SIDE - 2, lanes + 2 * LANE), jnp.float32)
+    k, width = pl.program_id(0), above_ref.shape[2]
+    starts = [
+        (jnp.maximum(k * lanes - LANE, 0), LANE),
+        (k * lanes, lanes),
+        (jnp.minimum((k + 1) * lanes, width - LANE), LANE),
+    ]
     body = lambda first, i, rows: joined(refs[first + 3 * (i // 2) : first + 3 * (i // 2) + 3], i % 2, rows)
-    beyond = lambda j, i: joined(refs[12 + 3 * j : 15 + 3 * j], i, slice(None))
+    beyond = lambda ref, i: jnp.concatenate(
+        [ref[i, :, pl.ds(pl.multiple_of(start, LANE), size)] for start, size in starts], axis=1
+    )
     top = [
-        jnp.concatenate([far, beyond(0, i), body(0, i, slice(0, kept + SIDE))], axis=0) for i in range(4)
+        jnp.concatenate([far, beyond(above_ref, i), body(0, i, slice(0, kept + SIDE))], axis=0)
+        for i in range(4)
     ]
     advance(top, out_ref, 0, jnp.where(edge_ref[0] == 1, SIDE, -1), None)
     bottom = [
-        jnp.concatenate([body(6, i, slice(tall - kept - SIDE, tall)), beyond(1, i), far], axis=0)
+        jnp.concatenate([body(6, i, slice(tall - kept - SIDE, tall)), beyond(below_ref, i), far], axis=0)
         for i in range(4)
     ]
     advance(bottom, out_ref, kept, None, jnp.where(edge_ref[1] == 1, SIDE + kept - 1, -1))
@@ -97,6 +111,10 @@
 
 def vmem():
     return pl.BlockSpec(memory_space=pltpu.VMEM)
+
+
+def resident(x):
+    return pltpu.with_memory_space_constraint(x, pltpu.VMEM)
 
 
 def around(count, height, width, row=0):
@@ -111,17 +129,19 @@
 def forecast_inner(ensemble, velocity, row0, kept):
     members, height, width = ensemble.shape
     per = BLOCK // LANE
+    beyond = jax.ShapeDtypeStruct((members + 2, 2, width), jnp.float32)
     return pl.pallas_call(
         functools.partial(inner_kernel, row0=row0, kept=kept),
         grid=(width // BLOCK,),
-        out_shape=jax.ShapeDtypeStruct((width // COLS, members, height, COLS), jnp.float32),
+        out_shape=[jax.ShapeDtypeStruct((width // COLS, members, kept, COLS), jnp.float32), beyond, beyond],
         in_specs=around(members, height, width) + around(2, height, width),
-        out_specs=pl.BlockSpec((per, members, kept, COLS), lambda k: (k, 0, 0, 0)),
+        out_specs=[pl.BlockSpec((per, members, kept, COLS), lambda k: (k, 0, 0, 0))]
+        + [pl.BlockSpec((members + 2, 2, BLOCK), lambda k: (0, 0, k))] * 2,
         name="forecast_inner",
     )(*[ensemble] * 3, *[velocity] * 3)
 
 
-def forecast_edge(edges, ensemble, velocity, above, below, kept, partial):
+def forecast_edge(edges, ensemble, velocity, above, below, kept):
     members, height, width = ensemble.shape
     per = BLOCK // LANE
     tall = kept + SIDE
@@ -129,16 +149,15 @@
     return pl.pallas_call(
         functools.partial(edge_kernel, kept=kept),
         grid=(width // BLOCK,),
-        out_shape=jax.ShapeDtypeStruct(partial.shape, jnp.float32),
+        out_shape=jax.ShapeDtypeStruct((width // COLS, members, 2 * kept, COLS), jnp.float32),
         in_specs=[pl.BlockSpec(memory_space=pltpu.SMEM)]
         + both(0)
         + both(height // tall - 1)
-        + around(4, 2, width) * 2
-        + [pl.BlockSpec(memory_space=pl.ANY)],
-        out_specs=pl.BlockSpec((per, members, 2 * kept, COLS), lambda k: (k, 0, height // (2 * kept) - 1, 0)),
-        input_output_aliases={19: 0},
+        + [vmem(), vmem()],
+        out_specs=pl.BlockSpec((per, members, 2 * kept, COLS), lambda k: (k, 0, 0, 0)),
         name="forecast_edge",
-    )(edges, *([ensemble] * 3 + [velocity] * 3) * 2, *[above] * 3, *[below] * 3, partial)
+        compiler_params=pltpu.CompilerParams(vmem_limit_bytes=48 << 20),
+    )(edges, *([ensemble] * 3 + [velocity] * 3) * 2, resident(above), resident(below))
 
 
 def split(x, parts=2):
@@ -174,7 +193,7 @@
     return ref.reshape(members * tiles, width).at[pl.ds(tile, members, stride=tiles), :]
 
 
-def analysis_kernel(obs_ref, x_ref, out_ref, *, groups, row_of):
+def analysis_kernel(obs_ref, x_ref, out_ref, *, groups, first, row_of):
     members = x_ref.shape[0]
     spare = members - 1.0
     wide = GROUP * members
@@ -272,7 +291,7 @@
             left = jnp.concatenate([left, left * first_half16], axis=1)
             a_high, a_low = split(anomalies[b])
             right = jnp.concatenate([a_high, a_high, a_low, jnp.zeros_like(a_low)], axis=0)
-            tile_of(out_ref, base + g * GROUP + b)[...] = mm(left, right) + averages[b]
+            tile_of(out_ref, first + base + g * GROUP + b)[...] = mm(left, right) + averages[b]
         yield
 
     running = [one(g) for g in range(groups)]
@@ -280,17 +299,24 @@
         running = [r for r in running if next(r, running) is None]
 
 
-def analyse(background, observations, groups, row_of):
-    _, rows, _ = background.shape
+def analyse(background, observations, groups, total, first, row_of, earlier=None):
+    members, rows, width = background.shape
+    kernel = functools.partial(analysis_kernel, groups=groups, first=first, row_of=row_of)
+    more = {}
+    if earlier is not None:
+        plain = kernel
+        kernel = lambda o, x, _, out: plain(o, x, out)
+        more = {"input_output_aliases": {2: 0}}
     return pl.pallas_call(
-        functools.partial(analysis_kernel, groups=groups, row_of=row_of),
+        kernel,
         grid=(rows // (groups * GROUP),),
-        out_shape=pltpu.VMEM(background.shape, jnp.float32),
-        in_specs=[vmem(), vmem()],
+        out_shape=pltpu.VMEM((members, total, width), jnp.float32),
+        in_specs=[vmem()] * (2 + len(more)),
         out_specs=vmem(),
         compiler_params=pltpu.CompilerParams(vmem_limit_bytes=32 << 20),
         name="analysis",
-    )(observations, pltpu.with_memory_space_constraint(background, pltpu.VMEM))
+        **more,
+    )(observations, resident(background), *([] if earlier is None else [resident(earlier)]))
 
 
 def exchange(x):
@@ -306,12 +332,9 @@
     edge = height // 8
     kept = height - 2 * edge
     groups = 2 * edge // GROUP
-    inner_steps = kept // (2 * edge)
-
-    def row_of(g):
-        step, half = pl.program_id(0), groups // 2
-        outer = g if g < half else height // GROUP - groups + g
-        return jnp.where(step < inner_steps, half + groups * step + g, outer)
+    half = groups // 2
+    inner_row = lambda g: half + groups * pl.program_id(0) + g
+    outer_row = lambda g: g if g < half else height // GROUP - groups + g
 
     columns = observed_column[:, 0]
     values = observed_value[:, 0]
@@ -322,12 +345,14 @@
     observations = observations.reshape(3, height // GROUP, LANE)
     edges = jnp.stack([here == 0, here == devices - 1]).astype(jnp.int32)
 
-    above = lax.ppermute(jnp.concatenate([ensemble[:, -2:], velocity[:, -2:]], axis=0), "tile", up)
-    below = lax.ppermute(jnp.concatenate([ensemble[:, :2], velocity[:, :2]], axis=0), "tile", down)
-    fields = forecast_inner(ensemble, velocity, edge, kept)
-    fields = forecast_edge(edges, ensemble, velocity, above, below, edge, fields)
-    fields = exchange(fields.reshape(-1, height, COLS))
-    done = analyse(fields, observations, groups, row_of)
+    first, to_next, to_last = forecast_inner(ensemble, velocity, edge, kept)
+    above = lax.ppermute(to_next, "tile", up)
+    below = lax.ppermute(to_last, "tile", down)
+    first = exchange(first.reshape(-1, kept, COLS))
+    second = forecast_edge(edges, ensemble, velocity, above, below, edge)
+    second = exchange(second.reshape(-1, 2 * edge, COLS))
+    done = analyse(first, observations, groups, height, 0, inner_row)
+    done = analyse(second, observations, groups, height, kept, outer_row, done)
     done = exchange(done)
     both = jnp.concatenate([done[:, kept : kept + edge], done[:, :kept], done[:, kept + edge :]], axis=1)
     both = both.reshape(-1, members, height, COLS)

time: 157 us -> 156 us (level)
  waiting for transfers between devices: 49.5 us -> 37.4 us
  starting transfers between devices: 17.9 us -> 27.9 us
  blocking collectives: 54 us -> 56.6 us
    all_to_all x1 -> x2, waiting for transfers between devices: 49.5 us -> 4.03 us  [exchange(): return lax.all_to_all(x, 'member', 0, 0, tiled=True)]
    ppermute x2, waiting for transfers between devices: 0.01 us -> 33.4 us  [the longest x1 32.3 us: per_device(): above = lax.ppermute(to_next, 'tile', up)]
    all_to_all x1 -> x2, starting transfers between devices: 12.2 us -> 21.7 us  [exchange(): return lax.all_to_all(x, 'member', 0, 0, tiled=True)]
    all_to_all x1, blocking collectives: 54 us -> 56.6 us  [exchange(): return lax.all_to_all(x, 'member', 0, 0, tiled=True)]
    pallas_call x1 -> x2, Pallas kernels: 16.4 us -> 16.9 us  [analyse(): pl.pallas_call(kernel, grid=(rows // (groups * GROUP),), out_shape=pltpu....]
  transfers between devices with their start and end apart: 3 -> 4, of which waited for: 1 -> 3; matrix products, arithmetic and copies ran while one was open for 1% -> 1% of each run, Pallas kernels for 4% -> 11%
where the time goes in v4:
time: 156 us; the launch traced here: 154 us
  blocking collectives  56.6 us (36%)
  waiting for transfers between devices  37.4 us (24%)
  starting transfers between devices  27.9 us (18%)
  Pallas kernels  27.6 us (18%)
  local copies, waits for them, and re-layouts  4.18 us (3%)
    all_to_all x1, blocking collectives, exchange(): return lax.all_to_all(x, 'member', 0, 0, tiled=True)  56.6 us
    ppermute x1, waiting for transfers between devices, per_device(): above = lax.ppermute(to_next, 'tile', up)  32.3 us
    all_to_all x2, starting transfers between devices, exchange(): return lax.all_to_all(x, 'member', 0, 0, tiled=True)  21.7 us
    pallas_call x2, Pallas kernels, analyse(): pl.pallas_call(kernel, grid=(rows // (groups * GROUP),), out_shape=pltpu....  16.9 us
    pallas_call x1, Pallas kernels, forecast_inner(): pl.pallas_call(functools.partial(inner_kernel, row0=row0, kept=kept), gri...  6.43 us
    pallas_call x1, Pallas kernels, forecast_edge(): pl.pallas_call(functools.partial(edge_kernel, kept=kept), grid=(width //...  4.27 us
    all_to_all x2, waiting for transfers between devices, exchange(): return lax.all_to_all(x, 'member', 0, 0, tiled=True)  4.03 us
    ppermute x1, starting transfers between devices, per_device(): below = lax.ppermute(to_last, 'tile', down)  3.53 us
  transfers between devices with their start and end apart: 4, of which 3 were waited for; matrix products, arithmetic and copies ran while one was open for 1% of the time, Pallas kernels for 11%

profile of v4, /device:TPU:7, one launch (start us, length us, event | category | flops | bytes accessed | tf_op | source)
XLA Modules:
  0.0 154.1 jit_solution(5096043528547011619)
XLA Ops:
  0.0 6.4 %forecast_inner.1 = (f32[32,2,48,128]{3,2,1,0:T(8,128)}, f32[4,2,4096]{2,1,0:T(2,128)}, f32[4,2,4096]{2,1,0:T(2,128)}) custom-call(f32[2,64,4096]{2,1,0:T(8,128)} %refs_8_.1, f32[2,64,4096]{2,1,0:T(8,128)} %refs_8_.1, f32[2,64,4096]{2,1,0:T(8,128)} %refs_8_.1, f32[2,64,4096]{2,1,0:T(8,128)} %refs_11_.1, f32[2,64,4096]{2,1,0:T(8,128)} %refs_11_.1, ...), custom_call_target="tpu_custom_call" | custom-call | tf_op jit(solution)/shard_map/forecast_inner/pallas_call | solution.py:133
  6.5 12.1 %all-to-all-start.1 = ((f32[64,48,128]{2,1,0:T(8,128)}), f32[64,48,128]{2,1,0:T(8,128)}, u32[]{:S(2)}, u32[]{:S(2)}) async-start(f32[64,48,128]{2,1,0:T(8,128)} %bitcast.25), calls=%async_computation.1 | async-start | bytes 3145728 | tf_op jit(solution)/shard_map/all_to_all | solution.py:323
  18.6 2.6 %collective-permute-start = (f32[4,2,4096]{2,1,0:T(2,128)S(1)}, f32[4,2,4096]{2,1,0:T(2,128)S(1)}, u32[]{:S(2)}, u32[]{:S(2)}) collective-permute-start(f32[4,2,4096]{2,1,0:T(2,128)S(1)} %copy-done.7), channel_id=1, source_target_pairs={{0,1},{1,2},{2,3},{3,4},{4,5},{5,6},{6,7},{8,9},{9,10},{10,11},{11... | collective-permute-start | bytes 393224 | tf_op jit(solution)/shard_map/ppermute | solution.py:349
  21.3 3.5 %collective-permute-start.1 = (f32[4,2,4096]{2,1,0:T(2,128)S(1)}, f32[4,2,4096]{2,1,0:T(2,128)S(1)}, u32[]{:S(2)}, u32[]{:S(2)}) collective-permute-start(f32[4,2,4096]{2,1,0:T(2,128)S(1)} %copy-done.6), channel_id=1, source_target_pairs={{1,0},{2,1},{3,2},{4,3},{5,4},{6,5},{7,6},{9,8},{10,9},{11,10},{12... | collective-permute-start | bytes 393224 | tf_op jit(solution)/shard_map/ppermute | solution.py:350
  24.8 0.1 add_convert_fusion.edge_ref
  24.9 32.3 %collective-permute-done.refs_12_ = f32[4,2,4096]{2,1,0:T(2,128)S(1)} collective-permute-done((f32[4,2,4096]{2,1,0:T(2,128)S(1)}, f32[4,2,4096]{2,1,0:T(2,128)S(1)}, u32[]{:S(2)}, u32[]{:S(2)}) %collective-permute-start) | collective-permute-done | bytes 131104 | tf_op jit(solution)/shard_map/ppermute | solution.py:349
  57.3 1.0 collective-permute-done.1.refs_13_
  58.3 1.6 %copy-done.1 = f32[2,64,4096]{2,1,0:T(8,128)S(1)} copy-done((f32[2,64,4096]{2,1,0:T(8,128)S(1)}, f32[2,64,4096]{2,1,0:T(8,128)}, u32[]{:S(2)}) %copy-start.1) | copy-done | bytes 2097176
  59.9 4.3 %forecast_edge.1 = f32[32,2,16,128]{3,2,1,0:T(8,128)} custom-call(s32[2]{0:T(128)S(1)} %add_convert_fusion.edge_ref, f32[2,64,4096]{2,1,0:T(8,128)S(1)} %copy-done, f32[2,64,4096]{2,1,0:T(8,128)S(1)} %copy-done, f32[2,64,4096]{2,1,0:T(8,128)S(1)} %copy-done, f32[2,64,4096]{2,1,0:T(8,128)S(1)} %copy-done.1, f32[2,64,4096]{2,1,0:T(8,128)S(1)} %copy-done.1, ...), custom_call_target="tpu_custom_call" | custom-call | tf_op jit(solution)/shard_map/forecast_edge/pallas_call | solution.py:149
  64.2 9.6 %all-to-all-start = ((f32[64,16,128]{2,1,0:T(8,128)}), f32[64,16,128]{2,1,0:T(8,128)S(1)}, u32[]{:S(2)}, u32[]{:S(2)}) async-start(f32[64,16,128]{2,1,0:T(8,128)} %bitcast.4), calls=%async_computation | async-start | bytes 1048576 | tf_op jit(solution)/shard_map/all_to_all | solution.py:323
  73.8 0.1 lt.28
  73.8 0.1 copy.13
  73.9 0.1 convert_element_type.40
  74.2 0.1 lt.30
  74.3 0.1 copy.15
  74.4 0.1 stack.16
  74.5 0.1 copy.14
  74.7 13.0 %analysis.2._ = f32[64,64,128]{2,1,0:T(8,128)S(1)} custom-call(f32[3,16,128]{2,1,0:T(8,128)S(1)} %pad_maximum_fusion.1.obs_ref.o, f32[64,48,128]{2,1,0:T(8,128)} %all-to-all-done.1.x_ref), custom_call_target="tpu_custom_call" | custom-call | tf_op jit(solution)/shard_map/analysis/pallas_call | solution.py:310
  87.7 4.0 %all-to-all-done.x = f32[64,16,128]{2,1,0:T(8,128)S(1)} async-done(((f32[64,16,128]{2,1,0:T(8,128)}), f32[64,16,128]{2,1,0:T(8,128)S(1)}, u32[]{:S(2)}, u32[]{:S(2)}) %all-to-all-start) | async-done | bytes 524320 | tf_op jit(solution)/shard_map/all_to_all | solution.py:323
  91.7 3.9 %analysis.3 = f32[64,64,128]{2,1,0:T(8,128)S(1)} custom-call(f32[3,16,128]{2,1,0:T(8,128)S(1)} %pad_maximum_fusion.1.obs_ref.o, f32[64,16,128]{2,1,0:T(8,128)S(1)} %all-to-all-done.x, f32[64,64,128]{2,1,0:T(8,128)S(1)} %analysis.2._), custom_call_target="tpu_custom_call", output_to_operand_aliasing={{}: (2, {})} | custom-call | tf_op jit(solution)/shard_map/analysis/pallas_call | solution.py:310
  95.6 56.6 %all_to_all.15 = f32[64,64,128]{2,1,0:T(8,128)S(1)} all-to-all(f32[64,64,128]{2,1,0:T(8,128)S(1)} %analysis.3), channel_id=1, replica_groups=mesh['member'=32,'tile'=8] {'member'}, dimensions={0} | all-to-all | bytes 4194304 | tf_op jit(solution)/shard_map/all_to_all | solution.py:323
  152.2 0.1 slice.13
  152.4 0.2 pad_maximum_fusion
  152.6 1.5 copy.19
  (28 shorter events, 0.4 us)
Async XLA Ops:
  6.4 12.2 %copy-start.7 = (f32[4,2,4096]{2,1,0:T(2,128)S(1)}, f32[4,2,4096]{2,1,0:T(2,128)}, u32[]{:S(2)}) copy-start(f32[4,2,4096]{2,1,0:T(2,128)} %get-tuple-element.8) | copy-start | bytes 393220
  6.4 14.8 %copy-start.6 = (f32[4,2,4096]{2,1,0:T(2,128)S(1)}, f32[4,2,4096]{2,1,0:T(2,128)}, u32[]{:S(2)}) copy-start(f32[4,2,4096]{2,1,0:T(2,128)} %get-tuple-element.9) | copy-start | bytes 393220
  6.5 51.8 %copy-start = (f32[2,64,4096]{2,1,0:T(8,128)S(1)}, f32[2,64,4096]{2,1,0:T(8,128)}, u32[]{:S(2)}) copy-start(f32[2,64,4096]{2,1,0:T(8,128)} %refs_8_.1) | copy-start | bytes 6291460
  6.5 57.7 %all-to-all-start.1 = ((f32[64,48,128]{2,1,0:T(8,128)}), f32[64,48,128]{2,1,0:T(8,128)}, u32[]{:S(2)}, u32[]{:S(2)}) async-start(f32[64,48,128]{2,1,0:T(8,128)} %bitcast.25), calls=%async_computation.1 | async-start | bytes 3145728 | tf_op jit(solution)/shard_map/all_to_all | solution.py:323
  18.6 38.7 %collective-permute-start = (f32[4,2,4096]{2,1,0:T(2,128)S(1)}, f32[4,2,4096]{2,1,0:T(2,128)S(1)}, u32[]{:S(2)}, u32[]{:S(2)}) collective-permute-start(f32[4,2,4096]{2,1,0:T(2,128)S(1)} %copy-done.7), channel_id=1, source_target_pairs={{0,1},{1,2},{2,3},{3,4},{4,5},{5,6},{6,7},{8,9},{9,10},{10,11},{11... | collective-permute-start | bytes 393224 | tf_op jit(solution)/shard_map/ppermute | solution.py:349
  21.3 37.0 %collective-permute-start.1 = (f32[4,2,4096]{2,1,0:T(2,128)S(1)}, f32[4,2,4096]{2,1,0:T(2,128)S(1)}, u32[]{:S(2)}, u32[]{:S(2)}) collective-permute-start(f32[4,2,4096]{2,1,0:T(2,128)S(1)} %copy-done.6), channel_id=1, source_target_pairs={{1,0},{2,1},{3,2},{4,3},{5,4},{6,5},{7,6},{9,8},{10,9},{11,10},{12... | collective-permute-start | bytes 393224 | tf_op jit(solution)/shard_map/ppermute | solution.py:350
  24.8 49.2 %copy-start.8 = (s32[64,1]{0,1:T(1,128)S(1)}, s32[64,1]{0,1:T(1,128)}, u32[]{:S(2)}) copy-start(s32[64,1]{0,1:T(1,128)} %param.11) | copy-start | bytes 772
  24.8 49.3 %copy-start.5 = (s32[64,1]{0,1:T(1,128)S(1)}, s32[64,1]{0,1:T(1,128)}, u32[]{:S(2)}) copy-start(s32[64,1]{0,1:T(1,128)} %param.10) | copy-start | bytes 772
  58.3 1.6 %copy-start.1 = (f32[2,64,4096]{2,1,0:T(8,128)S(1)}, f32[2,64,4096]{2,1,0:T(8,128)}, u32[]{:S(2)}) copy-start(f32[2,64,4096]{2,1,0:T(8,128)} %refs_11_.1) | copy-start | bytes 6291460
  59.9 14.0 %copy-start.4 = (s32[64,1,32]{0,2,1:T(8,128)S(1)}, s32[64,1,32]{0,2,1:T(8,128)}, u32[]{:S(2)}) copy-start(s32[64,1,32]{0,2,1:T(8,128)} %param.9) | copy-start | bytes 24580
  59.9 14.4 %copy-start.2 = (f32[64,1,32]{0,2,1:T(8,128)S(1)}, f32[64,1,32]{0,2,1:T(8,128)}, u32[]{:S(2)}) copy-start(f32[64,1,32]{0,2,1:T(8,128)} %param.12) | copy-start | bytes 24580
  59.9 14.6 %copy-start.3 = (f32[64,1,32]{0,2,1:T(8,128)S(1)}, f32[64,1,32]{0,2,1:T(8,128)}, u32[]{:S(2)}) copy-start(f32[64,1,32]{0,2,1:T(8,128)} %param.13) | copy-start | bytes 24580
  64.2 27.6 %all-to-all-start = ((f32[64,16,128]{2,1,0:T(8,128)}), f32[64,16,128]{2,1,0:T(8,128)S(1)}, u32[]{:S(2)}, u32[]{:S(2)}) async-start(f32[64,16,128]{2,1,0:T(8,128)} %bitcast.4), calls=%async_computation | async-start | bytes 1048576 | tf_op jit(solution)/shard_map/all_to_all | solution.py:323

commit v5 on v4

--- a/solution.py
+++ b/solution.py
@@ -5,8 +5,12 @@
 from jax import lax
 from jax.experimental import pallas as pl
 from jax.experimental.pallas import tpu as pltpu
+from jax.sharding import Mesh
 from jax.sharding import PartitionSpec as P
 
+CHIP = ("member_z", "member_y")
+CORE = "member_core"
+MEMBER = (*CHIP, CORE)
 COLS = 128
 SWEEPS = 6
 LANE = 128
@@ -53,60 +57,76 @@
     return [substep(substep(field, (slice(None), slice(None))), kept) for field in fields]
 
 
-def advance(pieces, out_ref, out_row, low_row, high_row):
+def advance(pieces, store, low_row, high_row):
     k, last = pl.program_id(0), pl.num_programs(0) - 1
     *fields, wind_x, wind_y = pieces
-    rows, lanes = wind_x.shape
+    _, lanes = wind_x.shape
     inside_left = jnp.where(k > 0, wind_y[:, :LANE], 0.0)
     inside_right = jnp.where(k < last, wind_y[:, lanes - LANE :], 0.0)
     wind_y = jnp.concatenate([inside_left, wind_y[:, LANE : lanes - LANE], inside_right], axis=1)
     first_col = jnp.where(k == 0, LANE, -1)
     last_col = jnp.where(k == last, lanes - LANE - 1, -1)
     new = stencil(fields, wind_x, wind_y, first_col, last_col, low_row, high_row)
+    count = lanes // LANE - 2
     for m, field in enumerate(new):
-        for t in range(field.shape[1] // LANE):
-            out_ref[t, m, pl.ds(out_row, rows - 2 * SIDE), :] = field[:, LANE * t : LANE * (t + 1)]
+        for t in range(count):
+            store(k * count, t, m, field[:, LANE * t : LANE * (t + 1)])
 
 
 def joined(refs, i, rows):
     return jnp.concatenate([ref[i, rows, :] for ref in refs], axis=1)
 
 
-def inner_kernel(*refs, row0, kept):
-    *refs, out_ref, up_ref, down_ref = refs
+def inner_kernel(edge_ref, *refs, row0, kept):
+    *refs, out_ref, near_ref, far_ref = refs
+    odd = edge_ref[2] == 1
     rows = slice(row0 - SIDE, row0 + kept + SIDE)
     for i in range(4):
         middle = refs[3 * (i // 2) + 1]
         height = middle.shape[1]
-        up_ref[i] = middle[i % 2, height - 2 : height, :]
-        down_ref[i] = middle[i % 2, 0:2, :]
-    advance([joined(refs[3 * (i // 2) : 3 * (i // 2) + 3], i % 2, rows) for i in range(4)], out_ref, 0, None, None)
+        span = pl.ds(pl.multiple_of(pl.program_id(0) * middle.shape[2], LANE), middle.shape[2])
+        first, last = middle[i % 2, 0:2, :], middle[i % 2, height - 2 : height, :]
+        near_ref[i, :, span] = jnp.where(odd, first, last)
+        far_ref[i, :, span] = jnp.where(odd, last, first)
+
+    def store(base, t, m, field):
+        out_ref[base + t, m] = field
+
+    advance([joined(refs[3 * (i // 2) : 3 * (i // 2) + 3], i % 2, rows) for i in range(4)], store, None, None)
 
 
 def edge_kernel(edge_ref, *refs, kept):
-    *refs, above_ref, below_ref, out_ref = refs
-    tall, lanes = refs[0].shape[1], out_ref.shape[0] * LANE
+    *refs, near_ref, far_ref, out_ref = refs
+    odd = edge_ref[2] == 1
+    tall, lanes = refs[0].shape[1], refs[1].shape[2]
     far = jnp.zeros((SIDE - 2, lanes + 2 * LANE), jnp.float32)
-    k, width = pl.program_id(0), above_ref.shape[2]
+    k, width = pl.program_id(0), near_ref.shape[2]
     starts = [
         (jnp.maximum(k * lanes - LANE, 0), LANE),
         (k * lanes, lanes),
         (jnp.minimum((k + 1) * lanes, width - LANE), LANE),
     ]
     body = lambda first, i, rows: joined(refs[first + 3 * (i // 2) : first + 3 * (i // 2) + 3], i % 2, rows)
-    beyond = lambda ref, i: jnp.concatenate(
-        [ref[i, :, pl.ds(pl.multiple_of(start, LANE), size)] for start, size in starts], axis=1
-    )
+    spans = [pl.ds(pl.multiple_of(start, LANE), size) for start, size in starts]
+    of = lambda ref, i: jnp.concatenate([ref[i, :, span] for span in spans], axis=1)
+    beyond = lambda above, i: jnp.where(odd == above, of(near_ref, i), of(far_ref, i))
     top = [
-        jnp.concatenate([far, beyond(above_ref, i), body(0, i, slice(0, kept + SIDE))], axis=0)
+        jnp.concatenate([far, beyond(True, i), body(0, i, slice(0, kept + SIDE))], axis=0)
         for i in range(4)
     ]
-    advance(top, out_ref, 0, jnp.where(edge_ref[0] == 1, SIDE, -1), None)
+
+    def store_at(row):
+        def store(base, t, m, field):
+            out_ref[(t % 2) ^ edge_ref[3], base // 2 + t // 2, m, pl.ds(row, kept), :] = field
+
+        return store
+
+    advance(top, store_at(0), jnp.where(edge_ref[0] == 1, SIDE, -1), None)
     bottom = [
-        jnp.concatenate([body(6, i, slice(tall - kept - SIDE, tall)), beyond(below_ref, i), far], axis=0)
+        jnp.concatenate([body(6, i, slice(tall - kept - SIDE, tall)), beyond(False, i), far], axis=0)
         for i in range(4)
     ]
-    advance(bottom, out_ref, kept, None, jnp.where(edge_ref[1] == 1, SIDE + kept - 1, -1))
+    advance(bottom, store_at(kept), None, jnp.where(edge_ref[1] == 1, SIDE + kept - 1, -1))
 
 
 def vmem():
@@ -126,38 +146,36 @@
     ]
 
 
-def forecast_inner(ensemble, velocity, row0, kept):
+def forecast_inner(edges, ensemble, velocity, row0, kept):
     members, height, width = ensemble.shape
-    per = BLOCK // LANE
-    beyond = jax.ShapeDtypeStruct((members + 2, 2, width), jnp.float32)
+    beyond = pltpu.VMEM((members + 2, 2, width), jnp.float32)
     return pl.pallas_call(
         functools.partial(inner_kernel, row0=row0, kept=kept),
         grid=(width // BLOCK,),
-        out_shape=[jax.ShapeDtypeStruct((width // COLS, members, kept, COLS), jnp.float32), beyond, beyond],
-        in_specs=around(members, height, width) + around(2, height, width),
-        out_specs=[pl.BlockSpec((per, members, kept, COLS), lambda k: (k, 0, 0, 0))]
-        + [pl.BlockSpec((members + 2, 2, BLOCK), lambda k: (0, 0, k))] * 2,
+        out_shape=[pltpu.VMEM((width // COLS, members, kept, COLS), jnp.float32), beyond, beyond],
+        in_specs=[pl.BlockSpec(memory_space=pltpu.SMEM)] + around(members, height, width) + around(2, height, width),
+        out_specs=[vmem()] * 3,
         name="forecast_inner",
-    )(*[ensemble] * 3, *[velocity] * 3)
-
-
-def forecast_edge(edges, ensemble, velocity, above, below, kept):
+        compiler_params=pltpu.CompilerParams(vmem_limit_bytes=24 << 20),
+    )(edges, *[ensemble] * 3, *[velocity] * 3)
+
+
+def forecast_edge(edges, ensemble, velocity, near, far, kept):
     members, height, width = ensemble.shape
-    per = BLOCK // LANE
     tall = kept + SIDE
     both = lambda row: around(members, tall, width, row) + around(2, tall, width, row)
     return pl.pallas_call(
         functools.partial(edge_kernel, kept=kept),
         grid=(width // BLOCK,),
-        out_shape=jax.ShapeDtypeStruct((width // COLS, members, 2 * kept, COLS), jnp.float32),
+        out_shape=pltpu.VMEM((2, width // COLS // 2, members, 2 * kept, COLS), jnp.float32),
         in_specs=[pl.BlockSpec(memory_space=pltpu.SMEM)]
         + both(0)
         + both(height // tall - 1)
         + [vmem(), vmem()],
-        out_specs=pl.BlockSpec((per, members, 2 * kept, COLS), lambda k: (k, 0, 0, 0)),
+        out_specs=vmem(),
         name="forecast_edge",
-        compiler_params=pltpu.CompilerParams(vmem_limit_bytes=48 << 20),
-    )(edges, *([ensemble] * 3 + [velocity] * 3) * 2, resident(above), resident(below))
+        compiler_params=pltpu.CompilerParams(vmem_limit_bytes=24 << 20),
+    )(edges, *([ensemble] * 3 + [velocity] * 3) * 2, resident(near), resident(far))
 
 
 def split(x, parts=2):
@@ -193,7 +211,7 @@
     return ref.reshape(members * tiles, width).at[pl.ds(tile, members, stride=tiles), :]
 
 
-def analysis_kernel(obs_ref, x_ref, out_ref, *, groups, first, row_of):
+def analysis_kernel(obs_ref, x_ref, out_ref, *, groups, first, row_of, blocked=False):
     members = x_ref.shape[0]
     spare = members - 1.0
     wide = GROUP * members
@@ -229,7 +247,7 @@
         row = pl.ds(row_of(g), 1)
         index = jnp.broadcast_to(obs_ref[0, row, :].astype(jnp.int32), (members, LANE))
         for b in range(GROUP):
-            x = tile_of(x_ref, base + g * GROUP + b)[...]
+            x = tile_of(x_ref, (0 if blocked else base) + g * GROUP + b)[...]
             average = jnp.mean(x, axis=0, keepdims=True)
             anomaly = x - average
             averages.append(average)
@@ -301,34 +319,36 @@
 
 def analyse(background, observations, groups, total, first, row_of, earlier=None):
     members, rows, width = background.shape
+    tiles = groups * GROUP
     kernel = functools.partial(analysis_kernel, groups=groups, first=first, row_of=row_of)
-    more = {}
-    if earlier is not None:
-        plain = kernel
-        kernel = lambda o, x, _, out: plain(o, x, out)
-        more = {"input_output_aliases": {2: 0}}
-    return pl.pallas_call(
-        kernel,
-        grid=(rows // (groups * GROUP),),
+    call = functools.partial(
+        pl.pallas_call,
+        grid=(rows // tiles,),
         out_shape=pltpu.VMEM((members, total, width), jnp.float32),
-        in_specs=[vmem()] * (2 + len(more)),
         out_specs=vmem(),
         compiler_params=pltpu.CompilerParams(vmem_limit_bytes=32 << 20),
         name="analysis",
-        **more,
-    )(observations, resident(background), *([] if earlier is None else [resident(earlier)]))
-
-
-def exchange(x):
-    return lax.all_to_all(x, "member", 0, 0, tiled=True)
+    )
+    if earlier is None:
+        field = pl.BlockSpec((members, tiles, width), lambda i: (0, i, 0))
+        background = pltpu.with_memory_space_constraint(background, pltpu.HBM)
+        return call(functools.partial(kernel, blocked=True), in_specs=[vmem(), field])(observations, background)
+    return call(
+        lambda o, x, _, out: kernel(o, x, out),
+        in_specs=[vmem()] * 3,
+        input_output_aliases={2: 0},
+    )(observations, resident(background), resident(earlier))
+
+
+def exchange(x, axes=MEMBER):
+    return lax.all_to_all(x, axes, 0, 0, tiled=True)
 
 
 def per_device(ensemble, velocity, observed_column, slot_count, radius, observed_value, error_variance):
     members, height, width = ensemble.shape
+    ensemble, velocity = (pltpu.with_memory_space_constraint(a, pltpu.HBM) for a in (ensemble, velocity))
     devices = lax.axis_size("tile")
     here = lax.axis_index("tile")
-    up = [(i, i + 1) for i in range(devices - 1)]
-    down = [(j, i) for i, j in up]
     edge = height // 8
     kept = height - 2 * edge
     groups = 2 * edge // GROUP
@@ -343,14 +363,18 @@
     root_weight = jnp.sqrt(active / (1.0 + offset * offset) / error_variance[:, 0])
     observations = jnp.stack([columns.astype(jnp.float32), root_weight, values])
     observations = observations.reshape(3, height // GROUP, LANE)
-    edges = jnp.stack([here == 0, here == devices - 1]).astype(jnp.int32)
-
-    first, to_next, to_last = forecast_inner(ensemble, velocity, edge, kept)
-    above = lax.ppermute(to_next, "tile", up)
-    below = lax.ppermute(to_last, "tile", down)
+
+    core = lax.axis_index(CORE)
+    edges = jnp.stack([here == 0, here == devices - 1, here % 2 == 1, core == 1]).astype(jnp.int32)
+    first, to_near, to_far = forecast_inner(edges, ensemble, velocity, edge, kept)
+    near = lax.ppermute(to_near, "tile", [(i, i ^ 1) for i in range(devices)])
     first = exchange(first.reshape(-1, kept, COLS))
-    second = forecast_edge(edges, ensemble, velocity, above, below, edge)
-    second = exchange(second.reshape(-1, 2 * edge, COLS))
+    inside = range(1, devices - 1)
+    far = lax.ppermute(to_far, "tile", [(i, i + 1 if i % 2 else i - 1) for i in inside])
+    second = forecast_edge(edges, ensemble, velocity, near, far, edge)
+    mine, swapped = second[0], lax.ppermute(second[1], CORE, [(0, 1), (1, 0)])
+    second = jnp.where(core == 0, jnp.stack([mine, swapped], axis=1), jnp.stack([swapped, mine], axis=1))
+    second = exchange(second.reshape(-1, 2 * edge, COLS), CHIP)
     done = analyse(first, observations, groups, height, 0, inner_row)
     done = analyse(second, observations, groups, height, kept, outer_row, done)
     done = exchange(done)
@@ -360,18 +384,19 @@
 
 
 def solution(mesh):
+    torus = Mesh(mesh.devices.reshape(4, 4, 2, mesh.shape["tile"]), (*MEMBER, "tile"))
     return jax.shard_map(
         per_device,
-        mesh=mesh,
+        mesh=torus,
         in_specs=(
-            P("member", "tile", None),
+            P(MEMBER, "tile", None),
             P(None, "tile", None),
-            P("tile", "member", None),
-            P("tile", "member"),
-            P("tile", "member"),
-            P("tile", "member", None),
-            P("tile", "member", None),
+            P("tile", MEMBER, None),
+            P("tile", MEMBER),
+            P("tile", MEMBER),
+            P("tile", MEMBER, None),
+            P("tile", MEMBER, None),
         ),
-        out_specs=P("member", "tile", None),
+        out_specs=P(MEMBER, "tile", None),
         check_vma=False,
     )

time: 156 us -> 157 us (level)
  waiting for transfers between devices: 37.4 us -> 42.2 us
  starting transfers between devices: 27.9 us -> 25.1 us
    ppermute x2 -> x3, waiting for transfers between devices: 33.4 us -> 38.9 us  [the longest x1 34.6 us: per_device(): near = lax.ppermute(to_near, 'tile', [(i, i ^ 1) for i in range(devices)])]
    ppermute x2 -> x3, starting transfers between devices: 6.18 us -> 4.49 us  [the longest x1 2.89 us: per_device(): lax.ppermute(to_far, 'tile', [(i, i + 1 if i % 2 else i - 1) for i in ins...]
    unnamed x20 -> x14, local copies, waits for them, and re-layouts: 1.8 us -> 0.21 us
  transfers between devices with their start and end apart: 4 -> 5, of which waited for: 3 -> 4; matrix products, arithmetic and copies ran while one was open for 1% -> 1% of each run, Pallas kernels for 11% -> 11%
where the time goes in v5:
time: 157 us; the launch traced here: 155 us
  blocking collectives  56.2 us (36%)
  waiting for transfers between devices  42.2 us (27%)
  Pallas kernels  27.5 us (18%)
  starting transfers between devices  25.1 us (16%)
  local copies, waits for them, and re-layouts  3.45 us (2%)
    all_to_all x1, blocking collectives, exchange(): return lax.all_to_all(x, axes, 0, 0, tiled=True)  56.2 us
    ppermute x1, waiting for transfers between devices, per_device(): near = lax.ppermute(to_near, 'tile', [(i, i ^ 1) for i in range(devices)])  34.6 us
    all_to_all x2, starting transfers between devices, exchange(): return lax.all_to_all(x, axes, 0, 0, tiled=True)  20.6 us
    pallas_call x1, Pallas kernels, analyse(): call(functools.partial(kernel, blocked=True), in_specs=[vmem(), field])  12.7 us
    pallas_call x1, Pallas kernels, forecast_inner(): pl.pallas_call(functools.partial(inner_kernel, row0=row0, kept=kept), gri...  6.71 us
    pallas_call x1, Pallas kernels, forecast_edge(): pl.pallas_call(functools.partial(edge_kernel, kept=kept), grid=(width //...  4.24 us
    pallas_call x1, Pallas kernels, analyse(): call(lambda o, x, _, out: kernel(o, x, out), in_specs=[vmem()] * 3, input...  3.86 us
    all_to_all x2, waiting for transfers between devices, exchange(): return lax.all_to_all(x, axes, 0, 0, tiled=True)  3.34 us
  transfers between devices with their start and end apart: 5, of which 4 were waited for; matrix products, arithmetic and copies ran while one was open for 1% of the time, Pallas kernels for 11%

profile of v5, /device:TPU:7, one launch (start us, length us, event | category | flops | bytes accessed | tf_op | source)
XLA Modules:
  0.0 155.0 jit_solution(203103371324476573)
XLA Ops:
  0.0 0.1 add_convert_fusion.edge_ref
  0.1 6.7 %forecast_inner.1 = (f32[32,2,48,128]{3,2,1,0:T(8,128)}, f32[4,2,4096]{2,1,0:T(2,128)S(1)}, f32[4,2,4096]{2,1,0:T(2,128)S(1)}) custom-call(s32[4]{0:T(128)S(1)} %add_convert_fusion.edge_ref, f32[2,64,4096]{2,1,0:T(8,128)} %refs_8_.1, f32[2,64,4096]{2,1,0:T(8,128)} %refs_8_.1, f32[2,64,4096]{2,1,0:T(8,128)} %refs_8_.1, f32[2,64,4096]{2,1,0:T(8,128)} %refs_11_.1, ...), custom_call_target="tpu_custom_call" | custom-call | tf_op jit(solution)/shard_map/forecast_inner/pallas_call | solution.py:152
  6.8 11.9 %all-to-all-start.1 = ((f32[64,48,128]{2,1,0:T(8,128)}), f32[64,48,128]{2,1,0:T(8,128)S(1)}, u32[]{:S(2)}, u32[]{:S(2)}) async-start(f32[64,48,128]{2,1,0:T(8,128)} %bitcast.10), calls=%async_computation.1 | async-start | bytes 3145728 | tf_op jit(solution)/shard_map/all_to_all | solution.py:344
  18.7 0.8 collective-permute-start
  19.5 2.9 %collective-permute-start.1 = (f32[4,2,4096]{2,1,0:T(2,128)S(1)}, f32[4,2,4096]{2,1,0:T(2,128)S(1)}, u32[]{:S(2)}, u32[]{:S(2)}) collective-permute-start(f32[4,2,4096]{2,1,0:T(2,128)S(1)} %get-tuple-element.9), channel_id=1, source_target_pairs={{1,2},{2,1},{3,4},{4,3},{5,6},{6,5},{9,10},{10,9},{11,12},{12,11},... | collective-permute-start | bytes 393224 | tf_op jit(solution)/shard_map/ppermute | solution.py:373
  22.4 34.6 %collective-permute-done.refs_12_ = f32[4,2,4096]{2,1,0:T(2,128)S(1)} collective-permute-done((f32[4,2,4096]{2,1,0:T(2,128)S(1)}, f32[4,2,4096]{2,1,0:T(2,128)S(1)}, u32[]{:S(2)}, u32[]{:S(2)}) %collective-permute-start) | collective-permute-done | bytes 131104 | tf_op jit(solution)/shard_map/ppermute | solution.py:370
  57.1 3.1 %collective-permute-done.1.refs_13_ = f32[4,2,4096]{2,1,0:T(2,128)S(1)} collective-permute-done((f32[4,2,4096]{2,1,0:T(2,128)S(1)}, f32[4,2,4096]{2,1,0:T(2,128)S(1)}, u32[]{:S(2)}, u32[]{:S(2)}) %collective-permute-start.1) | collective-permute-done | bytes 131104 | tf_op jit(solution)/shard_map/ppermute | solution.py:373
  60.1 4.2 %forecast_edge.1 = f32[2,16,2,16,128]{4,3,2,1,0:T(8,128)S(1)} custom-call(s32[4]{0:T(128)S(1)} %add_convert_fusion.edge_ref, f32[2,64,4096]{2,1,0:T(8,128)} %refs_8_.1, f32[2,64,4096]{2,1,0:T(8,128)} %refs_8_.1, f32[2,64,4096]{2,1,0:T(8,128)} %refs_8_.1, f32[2,64,4096]{2,1,0:T(8,128)} %refs_11_.1, f32[2,64,4096]{2,1,0:T(8,128)} %refs_11_.1, ...), custom_call_target="tpu_custom_call" | custom-call | tf_op jit(solution)/shard_map/forecast_edge/pallas_call | solution.py:167
  64.5 0.8 collective-permute-start.2
  65.3 1.2 collective-permute-done.2
  66.5 0.8 copy.17
  67.3 8.6 %all-to-all-start = ((f32[64,16,128]{2,1,0:T(8,128)}), f32[64,16,128]{2,1,0:T(8,128)S(1)}, u32[]{:S(2)}, u32[]{:S(2)}) async-start(f32[64,16,128]{2,1,0:T(8,128)} %bitcast.9), calls=%async_computation | async-start | bytes 1048576 | tf_op jit(solution)/shard_map/all_to_all | solution.py:344
  76.0 0.1 lt.34
  76.1 0.1 copy.14
  76.4 0.1 lt.36
  76.5 0.1 copy.16
  76.7 0.1 copy.15
  76.9 12.7 %analysis.2._ = f32[64,64,128]{2,1,0:T(8,128)S(1)} custom-call(f32[3,16,128]{2,1,0:T(8,128)S(1)} %pad_maximum_fusion.1.obs_ref.o, f32[64,48,128]{2,1,0:T(8,128)} %copy-done), custom_call_target="tpu_custom_call" | custom-call | tf_op jit(solution)/shard_map/analysis/pallas_call | solution.py:335
  89.6 3.3 %all-to-all-done.x = f32[64,16,128]{2,1,0:T(8,128)S(1)} async-done(((f32[64,16,128]{2,1,0:T(8,128)}), f32[64,16,128]{2,1,0:T(8,128)S(1)}, u32[]{:S(2)}, u32[]{:S(2)}) %all-to-all-start) | async-done | bytes 524320 | tf_op jit(solution)/shard_map/all_to_all | solution.py:344
  92.9 3.9 %analysis.3 = f32[64,64,128]{2,1,0:T(8,128)S(1)} custom-call(f32[3,16,128]{2,1,0:T(8,128)S(1)} %pad_maximum_fusion.1.obs_ref.o, f32[64,16,128]{2,1,0:T(8,128)S(1)} %all-to-all-done.x, f32[64,64,128]{2,1,0:T(8,128)S(1)} %analysis.2._), custom_call_target="tpu_custom_call", output_to_operand_aliasing={{}: (2, {})} | custom-call | tf_op jit(solution)/shard_map/analysis/pallas_call | solution.py:336
  96.8 56.2 %all_to_all.15 = f32[64,64,128]{2,1,0:T(8,128)S(1)} all-to-all(f32[64,64,128]{2,1,0:T(8,128)S(1)} %analysis.3), channel_id=1, replica_groups=mesh['member_z'=4,'member_y'=4,'member_core'=2,'tile'=8] {'member_z','me..., dimensions={0} | all-to-all | bytes 4194304 | tf_op jit(solution)/shard_map/all_to_all | solution.py:344
  153.1 0.1 slice.23
  153.2 0.2 pad_maximum_fusion
  153.4 1.5 copy.21
  (27 shorter events, 0.6 us)
Async XLA Ops:
  6.8 60.5 %all-to-all-start.1 = ((f32[64,48,128]{2,1,0:T(8,128)}), f32[64,48,128]{2,1,0:T(8,128)S(1)}, u32[]{:S(2)}, u32[]{:S(2)}) async-start(f32[64,48,128]{2,1,0:T(8,128)} %bitcast.10), calls=%async_computation.1 | async-start | bytes 3145728 | tf_op jit(solution)/shard_map/all_to_all | solution.py:344
  18.7 38.3 %collective-permute-start = (f32[4,2,4096]{2,1,0:T(2,128)S(1)}, f32[4,2,4096]{2,1,0:T(2,128)S(1)}, u32[]{:S(2)}, u32[]{:S(2)}) collective-permute-start(f32[4,2,4096]{2,1,0:T(2,128)S(1)} %get-tuple-element.8), channel_id=1, source_target_pairs={{0,1},{1,0},{2,3},{3,2},{4,5},{5,4},{6,7},{7,6},{8,9},{9,8},{10,11... | collective-permute-start | bytes 393224 | tf_op jit(solution)/shard_map/ppermute | solution.py:370
  19.5 40.6 %collective-permute-start.1 = (f32[4,2,4096]{2,1,0:T(2,128)S(1)}, f32[4,2,4096]{2,1,0:T(2,128)S(1)}, u32[]{:S(2)}, u32[]{:S(2)}) collective-permute-start(f32[4,2,4096]{2,1,0:T(2,128)S(1)} %get-tuple-element.9), channel_id=1, source_target_pairs={{1,2},{2,1},{3,4},{4,3},{5,6},{6,5},{9,10},{10,9},{11,12},{12,11},... | collective-permute-start | bytes 393224 | tf_op jit(solution)/shard_map/ppermute | solution.py:373
  64.4 11.7 %copy-start.3 = (s32[64,1,32]{0,2,1:T(8,128)S(1)}, s32[64,1,32]{0,2,1:T(8,128)}, u32[]{:S(2)}) copy-start(s32[64,1,32]{0,2,1:T(8,128)} %param.9) | copy-start | bytes 24580
  64.4 11.8 %copy-start.5 = (s32[64,1]{0,1:T(1,128)S(1)}, s32[64,1]{0,1:T(1,128)}, u32[]{:S(2)}) copy-start(s32[64,1]{0,1:T(1,128)} %param.11) | copy-start | bytes 772
  64.4 12.0 %copy-start.4 = (s32[64,1]{0,1:T(1,128)S(1)}, s32[64,1]{0,1:T(1,128)}, u32[]{:S(2)}) copy-start(s32[64,1]{0,1:T(1,128)} %param.10) | copy-start | bytes 772
  64.4 12.1 %copy-start.1 = (f32[64,1,32]{0,2,1:T(8,128)S(1)}, f32[64,1,32]{0,2,1:T(8,128)}, u32[]{:S(2)}) copy-start(f32[64,1,32]{0,2,1:T(8,128)} %param.12) | copy-start | bytes 24580
  64.4 12.3 %copy-start.2 = (f32[64,1,32]{0,2,1:T(8,128)S(1)}, f32[64,1,32]{0,2,1:T(8,128)}, u32[]{:S(2)}) copy-start(f32[64,1,32]{0,2,1:T(8,128)} %param.13) | copy-start | bytes 24580
  64.5 1.9 %collective-permute-start.2 = (f32[16,2,16,128]{3,2,1,0:T(8,128)S(1)}, f32[16,2,16,128]{3,2,1,0:T(8,128)S(1)}, u32[]{:S(2)}, u32[]{:S(2)}) collective-permute-start(f32[16,2,16,128]{3,2,1,0:T(8,128)S(1)} %get-tuple-element.14), channel_id=1, source_target_pairs={{0,8},{8,0},{1,9},{9,1},{2,10},{10,2},{3,11},{11,3},{4,12},{12,4},... | collective-permute-start | bytes 786440 | tf_op jit(solution)/shard_map/ppermute | solution.py:375
  67.3 9.6 %copy-start = (f32[64,48,128]{2,1,0:T(8,128)}, f32[64,48,128]{2,1,0:T(8,128)S(1)}, u32[]{:S(2)}) copy-start(f32[64,48,128]{2,1,0:T(8,128)S(1)} %all-to-all-done.1.x_ref) | copy-start | bytes 4718596
  67.3 25.6 %all-to-all-start = ((f32[64,16,128]{2,1,0:T(8,128)}), f32[64,16,128]{2,1,0:T(8,128)S(1)}, u32[]{:S(2)}, u32[]{:S(2)}) async-start(f32[64,16,128]{2,1,0:T(8,128)} %bitcast.9), calls=%async_computation | async-start | bytes 1048576 | tf_op jit(solution)/shard_map/all_to_all | solution.py:344

commit v6 on v5

--- a/solution.py
+++ b/solution.py
@@ -178,6 +178,24 @@
     )(edges, *([ensemble] * 3 + [velocity] * 3) * 2, resident(near), resident(far))
 
 
+def merge_kernel(edge_ref, both_ref, swapped_ref, out_ref):
+    core = edge_ref[3]
+    out_ref[:, core] = both_ref[0]
+    out_ref[:, 1 - core] = swapped_ref[...]
+
+
+def merge(edges, both, swapped):
+    chips, *rest = swapped.shape
+    return pl.pallas_call(
+        merge_kernel,
+        out_shape=pltpu.VMEM((chips, 2, *rest), jnp.float32),
+        in_specs=[pl.BlockSpec(memory_space=pltpu.SMEM), vmem(), vmem()],
+        out_specs=vmem(),
+        compiler_params=pltpu.CompilerParams(vmem_limit_bytes=125 << 19),
+        name="merge",
+    )(edges, resident(both), resident(swapped))
+
+
 def split(x, parts=2):
     out = []
     for _ in range(parts - 1):
@@ -372,8 +390,8 @@
     inside = range(1, devices - 1)
     far = lax.ppermute(to_far, "tile", [(i, i + 1 if i % 2 else i - 1) for i in inside])
     second = forecast_edge(edges, ensemble, velocity, near, far, edge)
-    mine, swapped = second[0], lax.ppermute(second[1], CORE, [(0, 1), (1, 0)])
-    second = jnp.where(core == 0, jnp.stack([mine, swapped], axis=1), jnp.stack([swapped, mine], axis=1))
+    swapped = lax.ppermute(second[1], CORE, [(0, 1), (1, 0)])
+    second = merge(edges, second, swapped)
     second = exchange(second.reshape(-1, 2 * edge, COLS), CHIP)
     done = analyse(first, observations, groups, height, 0, inner_row)
     done = analyse(second, observations, groups, height, kept, outer_row, done)

time: 157 us -> 161 us (1.025)
  local copies, waits for them, and re-layouts: 3.45 us -> 6.11 us
    unnamed x14 -> x22, local copies, waits for them, and re-layouts: 0.21 us -> 3.71 us
  transfers between devices with their start and end apart: 5 -> 5, of which waited for: 4 -> 4; matrix products, arithmetic and copies ran while one was open for 1% -> 1% of each run, Pallas kernels for 11% -> 12%
where the time goes in v6:
time: 161 us; the launch traced here: 159 us
  blocking collectives  56.2 us (35%)
  waiting for transfers between devices  42.2 us (26%)
  Pallas kernels  29 us (18%)
  starting transfers between devices  25 us (16%)
  local copies, waits for them, and re-layouts  6.11 us (4%)
    all_to_all x1, blocking collectives, exchange(): return lax.all_to_all(x, axes, 0, 0, tiled=True)  56.2 us
    ppermute x1, waiting for transfers between devices, per_device(): near = lax.ppermute(to_near, 'tile', [(i, i ^ 1) for i in range(devices)])  34.7 us
    all_to_all x2, starting transfers between devices, exchange(): return lax.all_to_all(x, axes, 0, 0, tiled=True)  20.6 us
    pallas_call x1, Pallas kernels, analyse(): call(functools.partial(kernel, blocked=True), in_specs=[vmem(), field])  12.7 us
    pallas_call x1, Pallas kernels, forecast_inner(): pl.pallas_call(functools.partial(inner_kernel, row0=row0, kept=kept), gri...  6.72 us
    pallas_call x1, Pallas kernels, forecast_edge(): pl.pallas_call(functools.partial(edge_kernel, kept=kept), grid=(width //...  4.24 us
    pallas_call x1, Pallas kernels, analyse(): call(lambda o, x, _, out: kernel(o, x, out), in_specs=[vmem()] * 3, input...  3.85 us
    unnamed x22, local copies, waits for them, and re-layouts  3.71 us
  transfers between devices with their start and end apart: 5, of which 4 were waited for; matrix products, arithmetic and copies ran while one was open for 1% of the time, Pallas kernels for 12%

profile of v6, /device:TPU:7, one launch (start us, length us, event | category | flops | bytes accessed | tf_op | source)
XLA Modules:
  0.0 159.0 jit_solution(12517949916833406530)
XLA Ops:
  0.1 6.7 %forecast_inner.1 = (f32[32,2,48,128]{3,2,1,0:T(8,128)}, f32[4,2,4096]{2,1,0:T(2,128)S(1)}, f32[4,2,4096]{2,1,0:T(2,128)S(1)}) custom-call(s32[4]{0:T(128)S(1)} %add_convert_fusion.edge_ref, f32[2,64,4096]{2,1,0:T(8,128)} %refs_8_.1, f32[2,64,4096]{2,1,0:T(8,128)} %refs_8_.1, f32[2,64,4096]{2,1,0:T(8,128)} %refs_8_.1, f32[2,64,4096]{2,1,0:T(8,128)} %refs_11_.1, ...), custom_call_target="tpu_custom_call" | custom-call | tf_op jit(solution)/shard_map/forecast_inner/pallas_call | solution.py:152
  6.8 12.0 %all-to-all-start.1 = ((f32[64,48,128]{2,1,0:T(8,128)}), f32[64,48,128]{2,1,0:T(8,128)}, u32[]{:S(2)}, u32[]{:S(2)}) async-start(f32[64,48,128]{2,1,0:T(8,128)} %bitcast.8), calls=%async_computation.1 | async-start | bytes 3145728 | tf_op jit(solution)/shard_map/all_to_all | solution.py:362
  18.8 0.8 collective-permute-start
  19.6 2.9 %collective-permute-start.1 = (f32[4,2,4096]{2,1,0:T(2,128)S(1)}, f32[4,2,4096]{2,1,0:T(2,128)S(1)}, u32[]{:S(2)}, u32[]{:S(2)}) collective-permute-start(f32[4,2,4096]{2,1,0:T(2,128)S(1)} %get-tuple-element.9), channel_id=1, source_target_pairs={{1,2},{2,1},{3,4},{4,3},{5,6},{6,5},{9,10},{10,9},{11,12},{12,11},... | collective-permute-start | bytes 393224 | tf_op jit(solution)/shard_map/ppermute | solution.py:391
  22.5 34.7 %collective-permute-done.refs_12_ = f32[4,2,4096]{2,1,0:T(2,128)S(1)} collective-permute-done((f32[4,2,4096]{2,1,0:T(2,128)S(1)}, f32[4,2,4096]{2,1,0:T(2,128)S(1)}, u32[]{:S(2)}, u32[]{:S(2)}) %collective-permute-start) | collective-permute-done | bytes 131104 | tf_op jit(solution)/shard_map/ppermute | solution.py:388
  57.2 3.0 %collective-permute-done.1.refs_13_ = f32[4,2,4096]{2,1,0:T(2,128)S(1)} collective-permute-done((f32[4,2,4096]{2,1,0:T(2,128)S(1)}, f32[4,2,4096]{2,1,0:T(2,128)S(1)}, u32[]{:S(2)}, u32[]{:S(2)}) %collective-permute-start.1) | collective-permute-done | bytes 131104 | tf_op jit(solution)/shard_map/ppermute | solution.py:391
  60.2 4.2 %forecast_edge.1.both_ref = f32[2,16,2,16,128]{4,3,2,1,0:T(8,128)S(1)} custom-call(s32[4]{0:T(128)S(1)} %add_convert_fusion.edge_ref, f32[2,64,4096]{2,1,0:T(8,128)} %refs_8_.1, f32[2,64,4096]{2,1,0:T(8,128)} %refs_8_.1, f32[2,64,4096]{2,1,0:T(8,128)} %refs_8_.1, f32[2,64,4096]{2,1,0:T(8,128)} %refs_11_.1, f32[2,64,4096]{2,1,0:T(8,128)} %refs_11_.1, ...), custom_call_target="tpu_custom_call" | custom-call | tf_op jit(solution)/shard_map/forecast_edge/pallas_call | solution.py:167
  64.5 0.8 copy-done
  65.3 0.7 collective-permute-start.2
  66.0 1.2 collective-permute-done.2.swapped_ref
  67.2 0.7 copy-done.2
  67.9 1.0 copy-done.1
  68.9 0.9 copy-done.3
  69.9 1.5 merge.1
  71.4 8.6 %all-to-all-start = ((f32[64,16,128]{2,1,0:T(8,128)}), f32[64,16,128]{2,1,0:T(8,128)S(1)}, u32[]{:S(2)}, u32[]{:S(2)}) async-start(f32[64,16,128]{2,1,0:T(8,128)} %bitcast.7), calls=%async_computation | async-start | bytes 1048576 | tf_op jit(solution)/shard_map/all_to_all | solution.py:362
  80.6 0.1 copy.15
  80.8 0.1 copy.14
  81.0 12.7 %analysis.2._ = f32[64,64,128]{2,1,0:T(8,128)S(1)} custom-call(f32[3,16,128]{2,1,0:T(8,128)S(1)} %pad_maximum_fusion.1.obs_ref.o, f32[64,48,128]{2,1,0:T(8,128)} %all-to-all-done.1.x_ref), custom_call_target="tpu_custom_call" | custom-call | tf_op jit(solution)/shard_map/analysis/pallas_call | solution.py:353
  93.7 3.3 %all-to-all-done.x = f32[64,16,128]{2,1,0:T(8,128)S(1)} async-done(((f32[64,16,128]{2,1,0:T(8,128)}), f32[64,16,128]{2,1,0:T(8,128)S(1)}, u32[]{:S(2)}, u32[]{:S(2)}) %all-to-all-start) | async-done | bytes 524320 | tf_op jit(solution)/shard_map/all_to_all | solution.py:362
  97.0 3.9 %analysis.3 = f32[64,64,128]{2,1,0:T(8,128)S(1)} custom-call(f32[3,16,128]{2,1,0:T(8,128)S(1)} %pad_maximum_fusion.1.obs_ref.o, f32[64,16,128]{2,1,0:T(8,128)S(1)} %all-to-all-done.x, f32[64,64,128]{2,1,0:T(8,128)S(1)} %analysis.2._), custom_call_target="tpu_custom_call", output_to_operand_aliasing={{}: (2, {})} | custom-call | tf_op jit(solution)/shard_map/analysis/pallas_call | solution.py:354
  100.9 56.2 %all_to_all.15 = f32[64,64,128]{2,1,0:T(8,128)S(1)} all-to-all(f32[64,64,128]{2,1,0:T(8,128)S(1)} %analysis.3), channel_id=1, replica_groups=mesh['member_z'=4,'member_y'=4,'member_core'=2,'tile'=8] {'member_z','me..., dimensions={0} | all-to-all | bytes 4194304 | tf_op jit(solution)/shard_map/all_to_all | solution.py:362
  157.1 0.1 slice.18
  157.3 0.2 pad_maximum_fusion
  157.5 1.5 copy.19
  (34 shorter events, 0.9 us)
Async XLA Ops:
  0.1 60.1 %copy-start.4 = (s32[4]{0:T(128)}, s32[4]{0:T(128)S(1)}, u32[]{:S(2)}) copy-start(s32[4]{0:T(128)S(1)} %add_convert_fusion.edge_ref) | copy-start | bytes 52
  6.8 64.6 %all-to-all-start.1 = ((f32[64,48,128]{2,1,0:T(8,128)}), f32[64,48,128]{2,1,0:T(8,128)}, u32[]{:S(2)}, u32[]{:S(2)}) async-start(f32[64,48,128]{2,1,0:T(8,128)} %bitcast.8), calls=%async_computation.1 | async-start | bytes 3145728 | tf_op jit(solution)/shard_map/all_to_all | solution.py:362
  18.8 38.4 %collective-permute-start = (f32[4,2,4096]{2,1,0:T(2,128)S(1)}, f32[4,2,4096]{2,1,0:T(2,128)S(1)}, u32[]{:S(2)}, u32[]{:S(2)}) collective-permute-start(f32[4,2,4096]{2,1,0:T(2,128)S(1)} %get-tuple-element.8), channel_id=1, source_target_pairs={{0,1},{1,0},{2,3},{3,2},{4,5},{5,4},{6,7},{7,6},{8,9},{9,8},{10,11... | collective-permute-start | bytes 393224 | tf_op jit(solution)/shard_map/ppermute | solution.py:388
  19.6 40.5 %collective-permute-start.1 = (f32[4,2,4096]{2,1,0:T(2,128)S(1)}, f32[4,2,4096]{2,1,0:T(2,128)S(1)}, u32[]{:S(2)}, u32[]{:S(2)}) collective-permute-start(f32[4,2,4096]{2,1,0:T(2,128)S(1)} %get-tuple-element.9), channel_id=1, source_target_pairs={{1,2},{2,1},{3,4},{4,3},{5,6},{6,5},{9,10},{10,9},{11,12},{12,11},... | collective-permute-start | bytes 393224 | tf_op jit(solution)/shard_map/ppermute | solution.py:391
  64.4 15.7 %copy-start.7 = (s32[64,1,32]{0,2,1:T(8,128)S(1)}, s32[64,1,32]{0,2,1:T(8,128)}, u32[]{:S(2)}) copy-start(s32[64,1,32]{0,2,1:T(8,128)} %param.9) | copy-start | bytes 24580
  64.4 15.9 %copy-start.9 = (s32[64,1]{0,1:T(1,128)S(1)}, s32[64,1]{0,1:T(1,128)}, u32[]{:S(2)}) copy-start(s32[64,1]{0,1:T(1,128)} %param.11) | copy-start | bytes 772
  64.4 16.0 %copy-start.8 = (s32[64,1]{0,1:T(1,128)S(1)}, s32[64,1]{0,1:T(1,128)}, u32[]{:S(2)}) copy-start(s32[64,1]{0,1:T(1,128)} %param.10) | copy-start | bytes 772
  64.4 16.2 %copy-start.5 = (f32[64,1,32]{0,2,1:T(8,128)S(1)}, f32[64,1,32]{0,2,1:T(8,128)}, u32[]{:S(2)}) copy-start(f32[64,1,32]{0,2,1:T(8,128)} %param.12) | copy-start | bytes 24580
  64.5 16.3 %copy-start.6 = (f32[64,1,32]{0,2,1:T(8,128)S(1)}, f32[64,1,32]{0,2,1:T(8,128)}, u32[]{:S(2)}) copy-start(f32[64,1,32]{0,2,1:T(8,128)} %param.13) | copy-start | bytes 24580
  64.5 0.8 copy-start
  65.3 1.8 %collective-permute-start.2 = (f32[16,2,16,128]{3,2,1,0:T(8,128)S(1)}, f32[16,2,16,128]{3,2,1,0:T(8,128)S(1)}, u32[]{:S(2)}, u32[]{:S(2)}) collective-permute-start(f32[16,2,16,128]{3,2,1,0:T(8,128)S(1)} %slice_bitcast_fusion), channel_id=1, source_target_pairs={{0,8},{8,0},{1,9},{9,1},{2,10},{10,2},{3,11},{11,3},{4,12},{12,4},... | collective-permute-start | bytes 786440 | tf_op jit(solution)/shard_map/ppermute | solution.py:393
  67.2 0.7 copy-start.2
  67.9 1.0 copy-start.1
  68.9 0.9 copy-start.3
  71.4 25.6 %all-to-all-start = ((f32[64,16,128]{2,1,0:T(8,128)}), f32[64,16,128]{2,1,0:T(8,128)S(1)}, u32[]{:S(2)}, u32[]{:S(2)}) async-start(f32[64,16,128]{2,1,0:T(8,128)} %bitcast.7), calls=%async_computation | async-start | bytes 1048576 | tf_op jit(solution)/shard_map/all_to_all | solution.py:362
